TPU v7x, 512 devices: a whole 4x4x16 slice. The times are simulated.
512 devices in a mesh: seq: 64 (over y, x, z_lo), tp: 8 (over z_hi, core).
Axes of the slice: x: 4, y: 4, z: 16 (z_hi: 4, z_lo: 4; z = z_hi * 4 + z_lo), core: 2. Of those that a mesh axis runs over, the one named last changes fastest.
Arguments:
- q_feat: bfloat16 [16384, 4096], P('seq', 'tp'), may hold values from -6 to 6
- k_feat: bfloat16 [16384, 4096], P('seq', 'tp'), may hold values from -6 to 6
- v_feat: bfloat16 [16384, 4096], P('seq', 'tp'), may hold values from -6 to 6
- stream: bfloat16 [16384, 4096], P('seq', 'tp'), may hold values from -6 to 6
- filters: float32 [4096, 16384], P(('tp', 'seq')), may hold values from -1.2 to 1.2
- w_out: bfloat16 [4096, 4096], P('tp', 'seq'), may hold values from -0.25 to 0.25
Outputs:
- mixed_out: bfloat16 [16384, 4096], P('seq', 'tp')
All inputs are finite; a program needn't handle non-finite values.
Results may differ from a plain program's by a relative error of at most 0.012.
Values may be sent and summed in bfloat16 or wider, within the bound.
No kernel may reach another device: no remote copies, remote signals or barrier semaphores. Data moves between devices by JAX's collectives and lax.ppermute only.
A program may use at most 64 MiB of HBM per device.

v0:
```python
import functools

import jax
import jax.numpy as jnp
import numpy as np
from jax import lax
from jax.experimental import pallas as pl
from jax.experimental.pallas import tpu as pltpu
from jax.sharding import Mesh
from jax.sharding import PartitionSpec as P


SEQ = ("y", "x", "zl")
ALL = ("y", "x", "zl", "zh", "c")
B = 256
N = 64
TOP = B * (N - 1) + 128
ROWS = TOP + B


def build_bank(h_ref, c, bank):
    lane = lax.broadcasted_iota(jnp.int32, (16, 128), 1)
    row = lax.broadcasted_iota(jnp.int32, (16, 128), 0)
    low = lane < row
    zero = jnp.zeros((16, 128), jnp.bfloat16)

    def put(w, val):
        v = TOP // 16 - w
        if 0 <= v < ROWS // 16:
            bank[pl.ds(16 * v, 16), :] = val

    rolled_before = jnp.zeros((16, 128), jnp.float32)
    before = zero
    for w in range(-16, -8):
        put(w, zero)
    for m in range(128):
        taps = jnp.broadcast_to(h_ref[c, pl.ds(m, 1), :], (16, 128))
        rolled = pltpu.roll(taps, 0, 1, stride=1, stride_axis=0)
        here = jnp.where(low, rolled_before, rolled).astype(jnp.bfloat16)
        rolled_before = rolled
        for j in range(1, 8):
            put(8 * (m - 1) + j, jnp.concatenate([before[:, 16 * j :], here[:, : 16 * j]], axis=1))
        put(8 * m, here)
        before = here


def conv_body(x_ref, h_ref, o_ref, padded, bank, acc0, acc1):
    padded[pl.ds(0, N), :] = jnp.zeros((N, B), jnp.float32)

    def channel(c, carry):
        padded[pl.ds(N, N), :] = x_ref[c].astype(jnp.float32)
        build_bank(h_ref, c, bank)
        for k in range(N):
            mxu, stage = k % 2, (k // 2) % 2
            r0 = TOP - B * k
            rhs = jnp.concatenate([bank[pl.ds(r0, B), :], bank[pl.ds(r0 - 128, B), :]], axis=1)
            pltpu.matmul_push_rhs(rhs, stage, mxu)
            lhs = padded[pl.ds(N - k, N), :].astype(jnp.bfloat16)
            pltpu.matmul_acc_lhs((acc0, acc1)[mxu], lhs, load_staged_rhs=stage)
        o_ref[c] = (pltpu.matmul_pop(acc0) + pltpu.matmul_pop(acc1)).astype(jnp.bfloat16)
        return carry

    lax.fori_loop(0, 8, channel, 0)


def conv_kernel(*refs):
    pl.run_scoped(
        functools.partial(conv_body, *refs),
        pltpu.ACC(0)((N, B), jnp.float32),
        pltpu.ACC(1)((N, B), jnp.float32),
    )


def causal_conv(x, taps):
    return pl.pallas_call(
        conv_kernel,
        out_shape=jax.ShapeDtypeStruct((8, N, B), jnp.bfloat16),
        in_specs=[pl.BlockSpec(memory_space=pltpu.VMEM)] * 2,
        out_specs=pl.BlockSpec(memory_space=pltpu.VMEM),
        scratch_shapes=[
            pltpu.VMEM((2 * N, B), jnp.float32),
            pltpu.VMEM((ROWS, 128), jnp.bfloat16),
        ],
        cost_estimate=pl.CostEstimate(flops=2**32, bytes_accessed=2**20, transcendentals=0),
        name="causal_conv",
    )(x, taps.reshape(8, 128, 128))


def mix_kernel(k_ref, v_ref, o_ref):
    mixed = k_ref[...].astype(jnp.float32) * v_ref[...].astype(jnp.float32)
    o_ref[...] = mixed.astype(jnp.bfloat16).T


def turn_kernel(q_ref, o_ref):
    o_ref[...] = q_ref[...].T


def small(kernel, *args):
    return pl.pallas_call(
        kernel,
        out_shape=jax.ShapeDtypeStruct((512, B), jnp.bfloat16),
        in_specs=[pl.BlockSpec(memory_space=pltpu.VMEM)] * len(args),
        out_specs=pl.BlockSpec(memory_space=pltpu.VMEM),
        cost_estimate=pl.CostEstimate(flops=2**18, bytes_accessed=2**19, transcendentals=0),
    )(*args)


def place(y, x, zl, zh, c):
    return (((y * 4 + x) * 4 + zl) * 4 + zh) * 2 + c


def weight_pairs():
    pairs = []
    for y in range(4):
        for x in range(4):
            for zl in range(4):
                for zh in range(4):
                    for c in range(2):
                        target = place(zh, 2 * c + x % 2, zl, y, x // 2)
                        pairs.append((place(y, x, zl, zh, c), target))
    return pairs


def rotate(values, axis, shift):
    return lax.ppermute(values, axis, [(i, (i + shift) % 4) for i in range(4)])


def swap(values):
    return lax.ppermute(values, "c", [(0, 1), (1, 0)])


def take(values, index):
    return lax.dynamic_index_in_dim(values, index.astype(jnp.uint32), 0, False)


def step(q_feat, k_feat, v_feat, stream, filters, w_out):
    y, zh, c = lax.axis_index("y"), lax.axis_index("zh"), lax.axis_index("c")
    mixed = small(mix_kernel, k_feat, v_feat).reshape(N, 8, B)
    sent = lax.all_to_all(mixed, SEQ, 0, 0, tiled=True)

    block = lax.ppermute(w_out.T, ALL, weight_pairs())
    block = jnp.broadcast_to(block[None], (16, 64, 512))
    row = lax.all_to_all(block, ("x", "zl"), 0, 0, tiled=True)
    row = row.reshape(2, 512, 512)
    weights = [row]
    for s in (1, -1, 2):
        weights.append(rotate(row, "y", s))

    conv = causal_conv(sent.transpose(1, 0, 2), filters)
    conv = conv.transpose(1, 0, 2)
    conv = lax.all_to_all(conv, SEQ, 0, 0, tiled=True).reshape(512, B)
    q_rows = small(turn_kernel, q_feat)
    gated = (q_rows.astype(jnp.float32) * conv.astype(jnp.float32)).astype(jnp.bfloat16)

    after = rotate(gated, "zh", 1)
    before = rotate(gated, "zh", -1)
    far_low = rotate(after[:256], "zh", 1)
    far_high = rotate(before[256:], "zh", -1)
    far = jnp.concatenate([far_low, far_high], axis=0)
    mine = jnp.stack([gated, after, far, before])
    other = jnp.stack([swap(p) for p in (gated, after, far, before)])

    total = stream.astype(jnp.float32)
    for shift, rows in zip((0, 1, -1, 2), weights):
        where = (zh - y + shift) & 3
        pair = take(mine, where), take(other, where)
        for core in range(2):
            part = jnp.where(c == core, *pair)
            total = total + lax.dot_general(
                part, rows[core], (((0,), (1,)), ((), ())), preferred_element_type=jnp.float32
            )
    return total.astype(jnp.bfloat16)


def solution(mesh):
    fine = Mesh(np.asarray(mesh.devices).reshape(4, 4, 4, 4, 2), ALL)
    tp = ("zh", "c")

    def run(*args):
        with jax.sharding.use_abstract_mesh(fine.abstract_mesh):
            return jax.shard_map(
                step,
                mesh=fine,
                in_specs=(P(SEQ, tp),) * 4 + (P(tp + SEQ, None), P(tp, SEQ)),
                out_specs=P(SEQ, tp),
                check_vma=False,
            )(*args)

    return run
```

profile of v0, /device:TPU:43, one launch (start us, length us, event | category | flops | bytes accessed | tf_op | source)
XLA Modules:
  0.0 213.1 jit_solution(1071240243602485521)
XLA Ops:
  0.0 1.9 shard_map.65
  1.9 11.0 %all-to-all-start = ((bf16[64,8,256]{2,1,0:T(8,128)(2,1)}), bf16[64,8,256]{2,1,0:T(8,128)(2,1)S(1)}, u32[]{:S(2)}, u32[]{:S(2)}) async-start(bf16[64,8,256]{2,1,0:T(8,128)(2,1)} %bitcast.73), calls=%async_computation | async-start | bytes 524288 | tf_op jit(solution)/shard_map/all_to_all | solution.py:139
  13.8 6.1 %all-to-all-done = bf16[64,8,256]{2,1,0:T(8,128)(2,1)S(1)} async-done(((bf16[64,8,256]{2,1,0:T(8,128)(2,1)}), bf16[64,8,256]{2,1,0:T(8,128)(2,1)S(1)}, u32[]{:S(2)}, u32[]{:S(2)}) %all-to-all-start) | async-done | bytes 262176 | tf_op jit(solution)/shard_map/all_to_all | solution.py:139
  20.7 20.3 %causal_conv.1 = bf16[8,64,256]{2,1,0:T(8,128)(2,1)} custom-call(bf16[8,64,256]{2,1,0:T(8,128)(2,1)} %bitcast.80, f32[8,128,128]{2,1,0:T(8,128)} %bitcast.79), custom_call_target="tpu_custom_call" | custom-call | flops 4294967296 | bytes 1048576 | tf_op jit(solution)/shard_map/causal_conv/pallas_call | solution.py:75
  41.0 1.8 copy.10
  42.8 10.4 %all-to-all-start.1 = ((bf16[64,8,256]{2,1,0:T(8,128)(2,1)}), bf16[64,8,256]{2,1,0:T(8,128)(2,1)S(1)}, u32[]{:S(2)}, u32[]{:S(2)}) async-start(bf16[64,8,256]{2,1,0:T(8,128)(2,1)} %copy.10), calls=%async_computation.1 | async-start | bytes 524288 | tf_op jit(solution)/shard_map/all_to_all | solution.py:151
  53.1 11.9 %collective-permute-start.8 = (bf16[64,512]{1,0:T(8,128)(2,1)S(1)}, bf16[64,512]{1,0:T(8,128)(2,1)S(1)}, u32[]{:S(2)}, u32[]{:S(2)}) collective-permute-start(bf16[64,512]{1,0:T(8,128)(2,1)S(1)} %bitcast.86), channel_id=1, source_target_pairs={{0,0},{1,64},{2,128},{3,192},{4,256},{5,320},{6,384},{7,448},{8,8}... | collective-permute-start | bytes 196616 | tf_op jit(solution)/shard_map/ppermute | solution.py:141
  65.0 5.8 %collective-permute-done.8 = bf16[64,512]{1,0:T(8,128)(2,1)S(1)} collective-permute-done((bf16[64,512]{1,0:T(8,128)(2,1)S(1)}, bf16[64,512]{1,0:T(8,128)(2,1)S(1)}, u32[]{:S(2)}, u32[]{:S(2)}) %collective-permute-start.8) | collective-permute-done | bytes 65568 | tf_op jit(solution)/shard_map/ppermute | solution.py:141
  71.9 7.5 %all-to-all-start.2 = ((bf16[16,64,512]{2,1,0:T(8,128)(2,1)}), bf16[16,64,512]{2,1,0:T(8,128)(2,1)S(1)}, u32[]{:S(2)}, u32[]{:S(2)}) async-start(bf16[16,64,512]{2,1,0:T(8,128)(2,1)} %broadcast_in_dim.2), calls=%async_computation.2 | async-start | bytes 2097152 | tf_op jit(solution)/shard_map/all_to_all | solution.py:143
  79.4 1.8 shard_map.64
  82.2 1.9 collective-permute-start
  84.1 9.2 %collective-permute-start.2 = (bf16[512,256]{1,0:T(8,128)(2,1)S(1)}, bf16[512,256]{1,0:T(8,128)(2,1)S(1)}, u32[]{:S(2)}, u32[]{:S(2)}) collective-permute-start(bf16[512,256]{1,0:T(8,128)(2,1)S(1)} %fusion.11), channel_id=1, source_target_pairs={{0,6},{2,0},{4,2},{6,4},{1,7},{3,1},{5,3},{7,5},{8,14},{10,8},{12,... | collective-permute-start | bytes 786440 | tf_op jit(solution)/shard_map/ppermute | solution.py:125
  93.3 46.6 %collective-permute-done = bf16[512,256]{1,0:T(8,128)(2,1)S(1)} collective-permute-done((bf16[512,256]{1,0:T(8,128)(2,1)S(1)}, bf16[512,256]{1,0:T(8,128)(2,1)S(1)}, u32[]{:S(2)}, u32[]{:S(2)}) %collective-permute-start) | collective-permute-done | bytes 262176 | tf_op jit(solution)/shard_map/ppermute | solution.py:125
  139.9 1.9 collective-permute-start.1
  141.9 7.3 %collective-permute-start.3 = (bf16[256,256]{1,0:T(8,128)(2,1)S(1)}, bf16[256,256]{1,0:T(8,128)(2,1)S(1)}, u32[]{:S(2)}, u32[]{:S(2)}) collective-permute-start(bf16[256,256]{1,0:T(8,128)(2,1)S(1)} %slice.43), channel_id=1, source_target_pairs={{0,6},{2,0},{4,2},{6,4},{1,7},{3,1},{5,3},{7,5},{8,14},{10,8},{12,... | collective-permute-start | bytes 393224 | tf_op jit(solution)/shard_map/ppermute | solution.py:125
  149.2 4.4 %collective-permute-start.4 = (bf16[512,256]{1,0:T(8,128)(2,1)S(1)}, bf16[512,256]{1,0:T(8,128)(2,1)S(1)}, u32[]{:S(2)}, u32[]{:S(2)}) collective-permute-start(bf16[512,256]{1,0:T(8,128)(2,1)S(1)} %fusion.11), channel_id=1, source_target_pairs={{0,1},{1,0},{2,3},{3,2},{4,5},{5,4},{6,7},{7,6},{8,9},{9,8},{10,11... | collective-permute-start | bytes 786440 | tf_op jit(solution)/shard_map/ppermute | solution.py:129
  153.6 1.9 collective-permute-start.7
  155.5 2.4 %collective-permute-start.5 = (bf16[512,256]{1,0:T(8,128)(2,1)S(1)}, bf16[512,256]{1,0:T(8,128)(2,1)S(1)}, u32[]{:S(2)}, u32[]{:S(2)}) collective-permute-start(bf16[512,256]{1,0:T(8,128)(2,1)S(1)} %collective-permute-done), channel_id=1, source_target_pairs={{0,1},{1,0},{2,3},{3,2},{4,5},{5,4},{6,7},{7,6},{8,9},{9,8},{10,11... | collective-permute-start | bytes 786440 | tf_op jit(solution)/shard_map/ppermute | solution.py:129
  158.0 1.9 collective-permute-start.6
  159.9 1.9 collective-permute-start.11
  162.2 5.3 %collective-permute-start.10 = (bf16[2,512,512]{2,1,0:T(8,128)(2,1)S(1)}, bf16[2,512,512]{2,1,0:T(8,128)(2,1)S(1)}, u32[]{:S(2)}, u32[]{:S(2)}) collective-permute-start(bf16[2,512,512]{2,1,0:T(8,128)(2,1)S(1)} %bitcast.69), channel_id=1, source_target_pairs={{0,384},{128,0},{256,128},{384,256},{1,385},{129,1},{257,129},{385... | collective-permute-start | bytes 3145736 | tf_op jit(solution)/shard_map/ppermute | solution.py:125
  167.6 1.9 collective-permute-start.9
  170.3 17.3 %collective-permute-done.11 = bf16[2,512,512]{2,1,0:T(8,128)(2,1)S(1)} collective-permute-done((bf16[2,512,512]{2,1,0:T(8,128)(2,1)S(1)}, bf16[2,512,512]{2,1,0:T(8,128)(2,1)S(1)}, u32[]{:S(2)}, u32[]{:S(2)}) %collective-permute-start.11) | collective-permute-done | bytes 1048608 | tf_op jit(solution)/shard_map/ppermute | solution.py:125
  188.3 22.6 %collective-permute-done.10 = bf16[2,512,512]{2,1,0:T(8,128)(2,1)S(1)} collective-permute-done((bf16[2,512,512]{2,1,0:T(8,128)(2,1)S(1)}, bf16[2,512,512]{2,1,0:T(8,128)(2,1)S(1)}, u32[]{:S(2)}, u32[]{:S(2)}) %collective-permute-start.10) | collective-permute-done | bytes 1048608 | tf_op jit(solution)/shard_map/ppermute | solution.py:125
  (35 shorter events, 7.8 us)
Async XLA Ops:
  0.0 12.9 %copy-start = (f32[8,16384]{1,0:T(8,128)S(1)}, f32[8,16384]{1,0:T(8,128)}, u32[]{:S(2)}) copy-start(f32[8,16384]{1,0:T(8,128)} %param.10) | copy-start | bytes 1572868
  1.9 18.0 %all-to-all-start = ((bf16[64,8,256]{2,1,0:T(8,128)(2,1)}), bf16[64,8,256]{2,1,0:T(8,128)(2,1)S(1)}, u32[]{:S(2)}, u32[]{:S(2)}) async-start(bf16[64,8,256]{2,1,0:T(8,128)(2,1)} %bitcast.73), calls=%async_computation | async-start | bytes 524288 | tf_op jit(solution)/shard_map/all_to_all | solution.py:139
  42.8 10.4 %copy-start.2 = (bf16[512,64]{0,1:T(8,128)(2,1)S(1)}, bf16[512,64]{0,1:T(8,128)(2,1)}, u32[]{:S(2)}) copy-start(bf16[512,64]{0,1:T(8,128)(2,1)} %param.11) | copy-start | bytes 196612
  42.8 28.0 %all-to-all-start.1 = ((bf16[64,8,256]{2,1,0:T(8,128)(2,1)}), bf16[64,8,256]{2,1,0:T(8,128)(2,1)S(1)}, u32[]{:S(2)}, u32[]{:S(2)}) async-start(bf16[64,8,256]{2,1,0:T(8,128)(2,1)} %copy.10), calls=%async_computation.1 | async-start | bytes 524288 | tf_op jit(solution)/shard_map/all_to_all | solution.py:151
  53.1 17.7 %collective-permute-start.8 = (bf16[64,512]{1,0:T(8,128)(2,1)S(1)}, bf16[64,512]{1,0:T(8,128)(2,1)S(1)}, u32[]{:S(2)}, u32[]{:S(2)}) collective-permute-start(bf16[64,512]{1,0:T(8,128)(2,1)S(1)} %bitcast.86), channel_id=1, source_target_pairs={{0,0},{1,64},{2,128},{3,192},{4,256},{5,320},{6,384},{7,448},{8,8}... | collective-permute-start | bytes 196616 | tf_op jit(solution)/shard_map/ppermute | solution.py:141
  71.9 88.0 %all-to-all-start.2 = ((bf16[16,64,512]{2,1,0:T(8,128)(2,1)}), bf16[16,64,512]{2,1,0:T(8,128)(2,1)S(1)}, u32[]{:S(2)}, u32[]{:S(2)}) async-start(bf16[16,64,512]{2,1,0:T(8,128)(2,1)} %broadcast_in_dim.2), calls=%async_computation.2 | async-start | bytes 2097152 | tf_op jit(solution)/shard_map/all_to_all | solution.py:143
  82.2 57.7 %collective-permute-start = (bf16[512,256]{1,0:T(8,128)(2,1)S(1)}, bf16[512,256]{1,0:T(8,128)(2,1)S(1)}, u32[]{:S(2)}, u32[]{:S(2)}) collective-permute-start(bf16[512,256]{1,0:T(8,128)(2,1)S(1)} %fusion.11), channel_id=1, source_target_pairs={{0,2},{2,4},{4,6},{6,0},{1,3},{3,5},{5,7},{7,1},{8,10},{10,12},{12... | collective-permute-start | bytes 786440 | tf_op jit(solution)/shard_map/ppermute | solution.py:125
  84.1 57.7 %collective-permute-start.2 = (bf16[512,256]{1,0:T(8,128)(2,1)S(1)}, bf16[512,256]{1,0:T(8,128)(2,1)S(1)}, u32[]{:S(2)}, u32[]{:S(2)}) collective-permute-start(bf16[512,256]{1,0:T(8,128)(2,1)S(1)} %fusion.11), channel_id=1, source_target_pairs={{0,6},{2,0},{4,2},{6,4},{1,7},{3,1},{5,3},{7,5},{8,14},{10,8},{12,... | collective-permute-start | bytes 786440 | tf_op jit(solution)/shard_map/ppermute | solution.py:125
  139.9 18.0 %collective-permute-start.1 = (bf16[256,256]{1,0:T(8,128)(2,1)S(1)}, bf16[256,256]{1,0:T(8,128)(2,1)S(1)}, u32[]{:S(2)}, u32[]{:S(2)}) collective-permute-start(bf16[256,256]{1,0:T(8,128)(2,1)S(1)} %slice.42), channel_id=1, source_target_pairs={{0,2},{2,4},{4,6},{6,0},{1,3},{3,5},{5,7},{7,1},{8,10},{10,12},{12... | collective-permute-start | bytes 393224 | tf_op jit(solution)/shard_map/ppermute | solution.py:125
  141.9 16.1 %collective-permute-start.3 = (bf16[256,256]{1,0:T(8,128)(2,1)S(1)}, bf16[256,256]{1,0:T(8,128)(2,1)S(1)}, u32[]{:S(2)}, u32[]{:S(2)}) collective-permute-start(bf16[256,256]{1,0:T(8,128)(2,1)S(1)} %slice.43), channel_id=1, source_target_pairs={{0,6},{2,0},{4,2},{6,4},{1,7},{3,1},{5,3},{7,5},{8,14},{10,8},{12,... | collective-permute-start | bytes 393224 | tf_op jit(solution)/shard_map/ppermute | solution.py:125
  149.2 12.8 %collective-permute-start.4 = (bf16[512,256]{1,0:T(8,128)(2,1)S(1)}, bf16[512,256]{1,0:T(8,128)(2,1)S(1)}, u32[]{:S(2)}, u32[]{:S(2)}) collective-permute-start(bf16[512,256]{1,0:T(8,128)(2,1)S(1)} %fusion.11), channel_id=1, source_target_pairs={{0,1},{1,0},{2,3},{3,2},{4,5},{5,4},{6,7},{7,6},{8,9},{9,8},{10,11... | collective-permute-start | bytes 786440 | tf_op jit(solution)/shard_map/ppermute | solution.py:129
  153.6 8.4 %collective-permute-start.7 = (bf16[512,256]{1,0:T(8,128)(2,1)S(1)}, bf16[512,256]{1,0:T(8,128)(2,1)S(1)}, u32[]{:S(2)}, u32[]{:S(2)}) collective-permute-start(bf16[512,256]{1,0:T(8,128)(2,1)S(1)} %collective-permute-done.2), channel_id=1, source_target_pairs={{0,1},{1,0},{2,3},{3,2},{4,5},{5,4},{6,7},{7,6},{8,9},{9,8},{10,11... | collective-permute-start | bytes 786440 | tf_op jit(solution)/shard_map/ppermute | solution.py:129
  155.5 6.5 %collective-permute-start.5 = (bf16[512,256]{1,0:T(8,128)(2,1)S(1)}, bf16[512,256]{1,0:T(8,128)(2,1)S(1)}, u32[]{:S(2)}, u32[]{:S(2)}) collective-permute-start(bf16[512,256]{1,0:T(8,128)(2,1)S(1)} %collective-permute-done), channel_id=1, source_target_pairs={{0,1},{1,0},{2,3},{3,2},{4,5},{5,4},{6,7},{7,6},{8,9},{9,8},{10,11... | collective-permute-start | bytes 786440 | tf_op jit(solution)/shard_map/ppermute | solution.py:129
  158.0 4.1 %collective-permute-start.6 = (bf16[512,256]{1,0:T(8,128)(2,1)S(1)}, bf16[512,256]{1,0:T(8,128)(2,1)S(1)}, u32[]{:S(2)}, u32[]{:S(2)}) collective-permute-start(bf16[512,256]{1,0:T(8,128)(2,1)S(1)} %constant_dynamic-update-slice_fusion), channel_id=1, source_target_pairs={{0,1},{1,0},{2,3},{3,2},{4,5},{5,4},{6,7},{7,6},{8,9},{9,8},{10,11... | collective-permute-start | bytes 786440 | tf_op jit(solution)/shard_map/ppermute | solution.py:129
  159.9 27.7 %collective-permute-start.11 = (bf16[2,512,512]{2,1,0:T(8,128)(2,1)S(1)}, bf16[2,512,512]{2,1,0:T(8,128)(2,1)S(1)}, u32[]{:S(2)}, u32[]{:S(2)}) collective-permute-start(bf16[2,512,512]{2,1,0:T(8,128)(2,1)S(1)} %bitcast.68), channel_id=1, source_target_pairs={{0,256},{128,384},{256,0},{384,128},{1,257},{129,385},{257,1},{385... | collective-permute-start | bytes 3145736 | tf_op jit(solution)/shard_map/ppermute | solution.py:125
  162.2 7.4 %copy-start.1 = (bf16[256,512]{1,0:T(8,128)(2,1)S(1)}, bf16[256,512]{1,0:T(8,128)(2,1)}, u32[]{:S(2)}) copy-start(bf16[256,512]{1,0:T(8,128)(2,1)} %param.9) | copy-start | bytes 786436
  162.2 48.7 %collective-permute-start.10 = (bf16[2,512,512]{2,1,0:T(8,128)(2,1)S(1)}, bf16[2,512,512]{2,1,0:T(8,128)(2,1)S(1)}, u32[]{:S(2)}, u32[]{:S(2)}) collective-permute-start(bf16[2,512,512]{2,1,0:T(8,128)(2,1)S(1)} %bitcast.69), channel_id=1, source_target_pairs={{0,384},{128,0},{256,128},{384,256},{1,385},{129,1},{257,129},{385... | collective-permute-start | bytes 3145736 | tf_op jit(solution)/shard_map/ppermute | solution.py:125
  167.6 44.1 %collective-permute-start.9 = (bf16[2,512,512]{2,1,0:T(8,128)(2,1)S(1)}, bf16[2,512,512]{2,1,0:T(8,128)(2,1)S(1)}, u32[]{:S(2)}, u32[]{:S(2)}) collective-permute-start(bf16[2,512,512]{2,1,0:T(8,128)(2,1)S(1)} %bitcast.70), channel_id=1, source_target_pairs={{0,128},{128,256},{256,384},{384,0},{1,129},{129,257},{257,385},{3... | collective-permute-start | bytes 3145736 | tf_op jit(solution)/shard_map/ppermute | solution.py:125
where the time goes:
time: 214 us; the launch traced here: 213 us
  waiting for transfers between devices  98.4 us (46%)
  starting transfers between devices  80.9 us (38%)
  Pallas kernels  24 us (11%)
  local copies, waits for them, and re-layouts  4.68 us (2%)
  matrix products  3.58 us (2%)
    ppermute x7, waiting for transfers between devices, rotate(): return lax.ppermute(values, axis, [(i, (i + shift) % 4) for i in range(4)])  86.5 us
    ppermute x7, starting transfers between devices, rotate(): return lax.ppermute(values, axis, [(i, (i + shift) % 4) for i in range(4)])  29.5 us
    pallas_call x1, Pallas kernels, causal_conv(): pl.pallas_call(conv_kernel, out_shape=jax.ShapeDtypeStruct((8, N, B), jnp...  20.3 us
    ppermute x1, starting transfers between devices, step(): block = lax.ppermute(w_out.T, ALL, weight_pairs())  11.9 us
    all_to_all x1, starting transfers between devices, step(): sent = lax.all_to_all(mixed, SEQ, 0, 0, tiled=True)  11 us
    ppermute x4, starting transfers between devices, swap(): return lax.ppermute(values, 'c', [(0, 1), (1, 0)])  10.7 us
    all_to_all x1, starting transfers between devices, step(): conv = lax.all_to_all(conv, SEQ, 0, 0, tiled=True).reshape(512, B)  10.4 us
    all_to_all x1, starting transfers between devices, step(): row = lax.all_to_all(block, ('x', 'zl'), 0, 0, tiled=True)  7.51 us
  transfers between devices with their start and end apart: 15, of which 5 were waited for; matrix products, arithmetic and copies ran while one was open for 2% of the time, Pallas kernels for 1%

commit v1 on v0

--- a/solution.py
+++ b/solution.py
@@ -14,76 +14,131 @@
 ALL = ("y", "x", "zl", "zh", "c")
 B = 256
 N = 64
-TOP = B * (N - 1) + 128
-ROWS = TOP + B
-
-
-def build_bank(h_ref, c, bank):
+
+
+def prep_kernel(h_ref, o_ref, ws):
+    row = lax.broadcasted_iota(jnp.int32, (16, 256), 0)
+    chunk = lax.broadcasted_iota(jnp.int32, (16, 256), 1) // 16
+    lane8 = lax.broadcasted_iota(jnp.int32, (8, 128), 1)
+    row8 = lax.broadcasted_iota(jnp.int32, (8, 128), 0)
+    low = lane8 < 16 * (row8 + 1)
+
+    def channel(c, carry):
+        for j in range(4):
+            x = h_ref[c, pl.ds(16 * j, 16), :]
+            for k in range(4):
+                n = 2**k
+                rows, chunks = (row & n) == 0, (chunk & n) == 0
+                up, down = pltpu.roll(x, 16 - n, 0), pltpu.roll(x, n, 0)
+                right, left = pltpu.roll(x, 16 * n, 1), pltpu.roll(x, 256 - 16 * n, 1)
+                x = jnp.where(rows, jnp.where(chunks, up, right), jnp.where(chunks, left, down))
+            ws[:, pl.ds(256 * (3 - j), 256)] = x
+        zero = jnp.zeros((8, 128), jnp.float32)
+        for g in range(16):
+            rolled = []
+            for m in range(8):
+                t = jnp.broadcast_to(ws[pl.ds(g, 1), pl.ds(128 * m, 128)], (8, 128))
+                rolled.append(pltpu.roll(t, 16, 1, stride=16, stride_axis=0))
+            rolled += [zero, zero]
+            q = [None] + [jnp.where(low, rolled[m - 1], rolled[m]) for m in range(1, 10)]
+            p = {m: jnp.concatenate([q[m], q[m - 1]], axis=0).astype(jnp.bfloat16) for m in range(2, 10)}
+            for d in range(4):
+                o_ref[c, d, g] = jnp.concatenate([p[8 - 2 * d], p[9 - 2 * d]], axis=1)
+        return carry
+
+    lax.fori_loop(0, 8, channel, 0)
+
+
+def prep(h):
+    return pl.pallas_call(
+        prep_kernel,
+        out_shape=jax.ShapeDtypeStruct((8, 4, 16, 16, 256), jnp.bfloat16),
+        in_specs=[pl.BlockSpec(memory_space=pltpu.VMEM)],
+        out_specs=pl.BlockSpec(memory_space=pltpu.VMEM),
+        scratch_shapes=[pltpu.VMEM((16, 1024), jnp.float32)],
+        cost_estimate=pl.CostEstimate(flops=2**26, bytes_accessed=2**22, transcendentals=0),
+        name="prep",
+    )(h.reshape(8, N, B))
+
+
+def conv_body(x_ref, p_ref, o_ref, xs, gx, next_even, next_odd, *accs):
+    xs[...] = x_ref[...].astype(jnp.float32)
     lane = lax.broadcasted_iota(jnp.int32, (16, 128), 1)
     row = lax.broadcasted_iota(jnp.int32, (16, 128), 0)
     low = lane < row
-    zero = jnp.zeros((16, 128), jnp.bfloat16)
-
-    def put(w, val):
-        v = TOP // 16 - w
-        if 0 <= v < ROWS // 16:
-            bank[pl.ds(16 * v, 16), :] = val
-
-    rolled_before = jnp.zeros((16, 128), jnp.float32)
-    before = zero
-    for w in range(-16, -8):
-        put(w, zero)
-    for m in range(128):
-        taps = jnp.broadcast_to(h_ref[c, pl.ds(m, 1), :], (16, 128))
-        rolled = pltpu.roll(taps, 0, 1, stride=1, stride_axis=0)
-        here = jnp.where(low, rolled_before, rolled).astype(jnp.bfloat16)
-        rolled_before = rolled
-        for j in range(1, 8):
-            put(8 * (m - 1) + j, jnp.concatenate([before[:, 16 * j :], here[:, : 16 * j]], axis=1))
-        put(8 * m, here)
-        before = here
-
-
-def conv_body(x_ref, h_ref, o_ref, padded, bank, acc0, acc1):
-    padded[pl.ds(0, N), :] = jnp.zeros((N, B), jnp.float32)
-
-    def channel(c, carry):
-        padded[pl.ds(N, N), :] = x_ref[c].astype(jnp.float32)
-        build_bank(h_ref, c, bank)
-        for k in range(N):
-            mxu, stage = k % 2, (k // 2) % 2
-            r0 = TOP - B * k
-            rhs = jnp.concatenate([bank[pl.ds(r0, B), :], bank[pl.ds(r0 - 128, B), :]], axis=1)
-            pltpu.matmul_push_rhs(rhs, stage, mxu)
-            lhs = padded[pl.ds(N - k, N), :].astype(jnp.bfloat16)
-            pltpu.matmul_acc_lhs((acc0, acc1)[mxu], lhs, load_staged_rhs=stage)
-        o_ref[c] = (pltpu.matmul_pop(acc0) + pltpu.matmul_pop(acc1)).astype(jnp.bfloat16)
-        return carry
-
-    lax.fori_loop(0, 8, channel, 0)
+    next_even[...] = jnp.zeros_like(next_even)
+    next_odd[...] = jnp.zeros_like(next_odd)
+    for c in range(8):
+        slot = gx[c % 2]
+        before = jnp.zeros((16, 128), jnp.float32)
+        for t in range(128):
+            b, half = t // 2, t % 2
+            tokens = jnp.broadcast_to(xs[b, pl.ds(c, 1), pl.ds(128 * half, 128)], (16, 128))
+            rolled = pltpu.roll(tokens, 0, 1, stride=1, stride_axis=0)
+            slot[b, :, pl.ds(128 * half, 128)] = jnp.where(low, before, rolled).astype(jnp.bfloat16)
+            before = rolled
+        for kt in range(4):
+            rhs = slot[pl.ds(16 * kt, 16)].reshape(256, 256)
+            for u in range(2):
+                pltpu.matmul_push_rhs(rhs, kt % 2, u)
+            for a in range(kt, 4):
+                for u in range(2):
+                    lhs = p_ref[c, a - kt, pl.ds(8 * u, 8)].reshape(128, 256)
+                    pltpu.matmul_acc_lhs(accs[2 * a + u], lhs, load_staged_rhs=kt % 2 if a == kt else None)
+        even, odd = [], []
+        for a in range(4):
+            z0, z1 = pltpu.matmul_pop(accs[2 * a]), pltpu.matmul_pop(accs[2 * a + 1])
+            s = [None] * 4
+            for g in range(8):
+                e = z0[16 * g : 16 * g + 16, :128]
+                o = z0[16 * g : 16 * g + 16, 128:] + z1[16 * g : 16 * g + 16, :128]
+                n = z1[16 * g : 16 * g + 16, 128:]
+                if g == 0:
+                    s = [e, o, n, None]
+                    continue
+                e, o, n = (pltpu.roll(v, 16 * g, 1) for v in (e, o, n))
+                mask = lane < 16 * g
+                s[0] = s[0] + jnp.where(mask, 0.0, e)
+                s[1] = s[1] + jnp.where(mask, e, o)
+                s[2] = s[2] + jnp.where(mask, o, n)
+                last = jnp.where(mask, n, 0.0)
+                s[3] = last if s[3] is None else s[3] + last
+            even.append(s[0])
+            odd.append(s[1])
+            next_even[pl.ds(16 * a + 1, 16), :] = s[2]
+            next_odd[pl.ds(16 * a + 1, 16), :] = s[3]
+        for a in range(4):
+            rows = pl.ds(16 * a, 16)
+            xs[rows, c, pl.ds(0, 128)] = even[a] + next_even[rows, :]
+            xs[rows, c, pl.ds(128, 128)] = odd[a] + next_odd[rows, :]
+    o_ref[...] = xs[...].astype(jnp.bfloat16)
 
 
 def conv_kernel(*refs):
-    pl.run_scoped(
-        functools.partial(conv_body, *refs),
-        pltpu.ACC(0)((N, B), jnp.float32),
-        pltpu.ACC(1)((N, B), jnp.float32),
-    )
-
-
-def causal_conv(x, taps):
+    pl.run_scoped(functools.partial(wrap, refs), *[pltpu.ACC(u)((128, B), jnp.float32) for _ in range(4) for u in range(2)])
+
+
+def wrap(refs, *accs):
+    x_ref, p_ref, o_ref, xs, g0, g1, ne, no = refs
+    conv_body(x_ref, p_ref, o_ref, xs, (g0, g1), ne, no, *accs)
+
+
+def causal_conv(x, p):
     return pl.pallas_call(
         conv_kernel,
-        out_shape=jax.ShapeDtypeStruct((8, N, B), jnp.bfloat16),
+        out_shape=jax.ShapeDtypeStruct((N, 8, B), jnp.bfloat16),
         in_specs=[pl.BlockSpec(memory_space=pltpu.VMEM)] * 2,
         out_specs=pl.BlockSpec(memory_space=pltpu.VMEM),
         scratch_shapes=[
-            pltpu.VMEM((2 * N, B), jnp.float32),
-            pltpu.VMEM((ROWS, 128), jnp.bfloat16),
+            pltpu.VMEM((N, 8, B), jnp.float32),
+            pltpu.VMEM((N, 16, B), jnp.bfloat16),
+            pltpu.VMEM((N, 16, B), jnp.bfloat16),
+            pltpu.VMEM((N + 8, 128), jnp.float32),
+            pltpu.VMEM((N + 8, 128), jnp.float32),
         ],
-        cost_estimate=pl.CostEstimate(flops=2**32, bytes_accessed=2**20, transcendentals=0),
+        cost_estimate=pl.CostEstimate(flops=2**32, bytes_accessed=2**22, transcendentals=0),
         name="causal_conv",
-    )(x, taps.reshape(8, 128, 128))
+    )(x, p)
 
 
 def mix_kernel(k_ref, v_ref, o_ref):
@@ -146,8 +201,8 @@
     for s in (1, -1, 2):
         weights.append(rotate(row, "y", s))
 
-    conv = causal_conv(sent.transpose(1, 0, 2), filters)
-    conv = conv.transpose(1, 0, 2)
+    taps = prep(filters)
+    conv = causal_conv(sent, taps)
     conv = lax.all_to_all(conv, SEQ, 0, 0, tiled=True).reshape(512, B)
     q_rows = small(turn_kernel, q_feat)
     gated = (q_rows.astype(jnp.float32) * conv.astype(jnp.float32)).astype(jnp.bfloat16)

time: 214 us -> 203 us (0.949)
  the two profiles are of different devices: /device:TPU:43 before, /device:TPU:34 now
where the time goes in v1:
time: 203 us; the launch traced here: 202 us
  waiting for transfers between devices  98.6 us (49%)
  starting transfers between devices  77.9 us (38%)
  Pallas kernels  16.1 us (8%)
  local copies, waits for them, and re-layouts  3.94 us (2%)
  matrix products  3.59 us (2%)
    ppermute x7, waiting for transfers between devices, rotate(): return lax.ppermute(values, axis, [(i, (i + shift) % 4) for i in range(4)])  87.3 us
    ppermute x7, starting transfers between devices, rotate(): return lax.ppermute(values, axis, [(i, (i + shift) % 4) for i in range(4)])  42.2 us
    all_to_all x1, starting transfers between devices, step(): sent = lax.all_to_all(mixed, SEQ, 0, 0, tiled=True)  11.6 us
    all_to_all x1, waiting for transfers between devices, step(): conv = lax.all_to_all(conv, SEQ, 0, 0, tiled=True).reshape(512, B)  9.13 us
    ppermute x4, starting transfers between devices, swap(): return lax.ppermute(values, 'c', [(0, 1), (1, 0)])  8.65 us
    all_to_all x1, starting transfers between devices, step(): conv = lax.all_to_all(conv, SEQ, 0, 0, tiled=True).reshape(512, B)  8.44 us
    all_to_all x1, starting transfers between devices, step(): row = lax.all_to_all(block, ('x', 'zl'), 0, 0, tiled=True)  6.34 us
    pallas_call x1, Pallas kernels, causal_conv(): pl.pallas_call(conv_kernel, out_shape=jax.ShapeDtypeStruct((N, 8, B), jnp...  6.27 us
  transfers between devices with their start and end apart: 15, of which 5 were waited for; matrix products, arithmetic and copies ran while one was open for 3% of the time, Pallas kernels for 4%

profile of v1, /device:TPU:34, one launch (start us, length us, event | category | flops | bytes accessed | tf_op | source)
XLA Modules:
  0.0 201.8 jit_solution(12197713869380072189)
XLA Ops:
  0.0 1.9 shard_map.65
  1.9 11.6 %all-to-all-start = ((bf16[64,8,256]{2,1,0:T(8,128)(2,1)}), bf16[64,8,256]{2,1,0:T(8,128)(2,1)S(1)}, u32[]{:S(2)}, u32[]{:S(2)}) async-start(bf16[64,8,256]{2,1,0:T(8,128)(2,1)} %bitcast.70), calls=%async_computation | async-start | bytes 524288 | tf_op jit(solution)/shard_map/all_to_all | solution.py:194
  13.5 2.0 copy.9
  15.5 6.2 %prep.1.refs_1_ = bf16[8,4,16,16,256]{4,3,2,1,0:T(8,128)(2,1)} custom-call(f32[8,64,256]{2,1,0:T(8,128)} %bitcast.67), custom_call_target="tpu_custom_call" | custom-call | flops 67108864 | bytes 4194304 | tf_op jit(solution)/shard_map/prep/pallas_call | solution.py:53
  21.7 2.2 %all-to-all-done.refs_0_ = bf16[64,8,256]{2,1,0:T(8,128)(2,1)S(1)} async-done(((bf16[64,8,256]{2,1,0:T(8,128)(2,1)}), bf16[64,8,256]{2,1,0:T(8,128)(2,1)S(1)}, u32[]{:S(2)}, u32[]{:S(2)}) %all-to-all-start) | async-done | bytes 262176 | tf_op jit(solution)/shard_map/all_to_all | solution.py:194
  24.6 6.3 %causal_conv.1 = bf16[64,8,256]{2,1,0:T(8,128)(2,1)} custom-call(bf16[64,8,256]{2,1,0:T(8,128)(2,1)} %copy-done.1, bf16[8,4,16,16,256]{4,3,2,1,0:T(8,128)(2,1)} %prep.1.refs_1_), custom_call_target="tpu_custom_call" | custom-call | flops 4294967296 | bytes 4194304 | tf_op jit(solution)/shard_map/causal_conv/pallas_call | solution.py:127
  30.8 8.4 %all-to-all-start.1 = ((bf16[64,8,256]{2,1,0:T(8,128)(2,1)}), bf16[64,8,256]{2,1,0:T(8,128)(2,1)S(1)}, u32[]{:S(2)}, u32[]{:S(2)}) async-start(bf16[64,8,256]{2,1,0:T(8,128)(2,1)} %causal_conv.1), calls=%async_computation.1 | async-start | bytes 524288 | tf_op jit(solution)/shard_map/all_to_all | solution.py:206
  40.0 9.1 %all-to-all-done.1 = bf16[64,8,256]{2,1,0:T(8,128)(2,1)S(1)} async-done(((bf16[64,8,256]{2,1,0:T(8,128)(2,1)}), bf16[64,8,256]{2,1,0:T(8,128)(2,1)S(1)}, u32[]{:S(2)}, u32[]{:S(2)}) %all-to-all-start.1) | async-done | bytes 262176 | tf_op jit(solution)/shard_map/all_to_all | solution.py:206
  50.2 6.3 %all-to-all-start.2 = ((bf16[16,64,512]{2,1,0:T(8,128)(2,1)}), bf16[16,64,512]{2,1,0:T(8,128)(2,1)S(1)}, u32[]{:S(2)}, u32[]{:S(2)}) async-start(bf16[16,64,512]{2,1,0:T(8,128)(2,1)} %broadcast_in_dim.2), calls=%async_computation.2 | async-start | bytes 2097152 | tf_op jit(solution)/shard_map/all_to_all | solution.py:198
  56.5 1.8 shard_map.64
  59.4 17.0 %collective-permute-start = (bf16[512,256]{1,0:T(8,128)(2,1)S(1)}, bf16[512,256]{1,0:T(8,128)(2,1)S(1)}, u32[]{:S(2)}, u32[]{:S(2)}) collective-permute-start(bf16[512,256]{1,0:T(8,128)(2,1)S(1)} %fusion.11), channel_id=1, source_target_pairs={{0,2},{2,4},{4,6},{6,0},{1,3},{3,5},{5,7},{7,1},{8,10},{10,12},{12... | collective-permute-start | bytes 786440 | tf_op jit(solution)/shard_map/ppermute | solution.py:180
  76.3 1.9 collective-permute-start.2
  78.3 45.5 %collective-permute-done = bf16[512,256]{1,0:T(8,128)(2,1)S(1)} collective-permute-done((bf16[512,256]{1,0:T(8,128)(2,1)S(1)}, bf16[512,256]{1,0:T(8,128)(2,1)S(1)}, u32[]{:S(2)}, u32[]{:S(2)}) %collective-permute-start) | collective-permute-done | bytes 262176 | tf_op jit(solution)/shard_map/ppermute | solution.py:180
  123.8 1.9 collective-permute-start.1
  125.8 7.9 %collective-permute-start.3 = (bf16[256,256]{1,0:T(8,128)(2,1)S(1)}, bf16[256,256]{1,0:T(8,128)(2,1)S(1)}, u32[]{:S(2)}, u32[]{:S(2)}) collective-permute-start(bf16[256,256]{1,0:T(8,128)(2,1)S(1)} %slice.43), channel_id=1, source_target_pairs={{0,6},{2,0},{4,2},{6,4},{1,7},{3,1},{5,3},{7,5},{8,14},{10,8},{12,... | collective-permute-start | bytes 393224 | tf_op jit(solution)/shard_map/ppermute | solution.py:180
  133.7 1.9 collective-permute-start.4
  135.6 2.4 %collective-permute-start.5 = (bf16[512,256]{1,0:T(8,128)(2,1)S(1)}, bf16[512,256]{1,0:T(8,128)(2,1)S(1)}, u32[]{:S(2)}, u32[]{:S(2)}) collective-permute-start(bf16[512,256]{1,0:T(8,128)(2,1)S(1)} %collective-permute-done), channel_id=1, source_target_pairs={{0,1},{1,0},{2,3},{3,2},{4,5},{5,4},{6,7},{7,6},{8,9},{9,8},{10,11... | collective-permute-start | bytes 786440 | tf_op jit(solution)/shard_map/ppermute | solution.py:184
  138.0 1.9 collective-permute-start.7
  140.0 2.4 %collective-permute-start.6 = (bf16[512,256]{1,0:T(8,128)(2,1)S(1)}, bf16[512,256]{1,0:T(8,128)(2,1)S(1)}, u32[]{:S(2)}, u32[]{:S(2)}) collective-permute-start(bf16[512,256]{1,0:T(8,128)(2,1)S(1)} %constant_dynamic-update-slice_fusion), channel_id=1, source_target_pairs={{0,1},{1,0},{2,3},{3,2},{4,5},{5,4},{6,7},{7,6},{8,9},{9,8},{10,11... | collective-permute-start | bytes 786440 | tf_op jit(solution)/shard_map/ppermute | solution.py:184
  142.5 4.0 %collective-permute-start.10 = (bf16[2,512,512]{2,1,0:T(8,128)(2,1)S(1)}, bf16[2,512,512]{2,1,0:T(8,128)(2,1)S(1)}, u32[]{:S(2)}, u32[]{:S(2)}) collective-permute-start(bf16[2,512,512]{2,1,0:T(8,128)(2,1)S(1)} %bitcast.64), channel_id=1, source_target_pairs={{0,384},{128,0},{256,128},{384,256},{1,385},{129,1},{257,129},{385... | collective-permute-start | bytes 3145736 | tf_op jit(solution)/shard_map/ppermute | solution.py:180
  146.8 3.6 %collective-permute-start.9 = (bf16[2,512,512]{2,1,0:T(8,128)(2,1)S(1)}, bf16[2,512,512]{2,1,0:T(8,128)(2,1)S(1)}, u32[]{:S(2)}, u32[]{:S(2)}) collective-permute-start(bf16[2,512,512]{2,1,0:T(8,128)(2,1)S(1)} %bitcast.65), channel_id=1, source_target_pairs={{0,128},{128,256},{256,384},{384,0},{1,129},{129,257},{257,385},{3... | collective-permute-start | bytes 3145736 | tf_op jit(solution)/shard_map/ppermute | solution.py:180
  150.5 5.8 %collective-permute-start.11 = (bf16[2,512,512]{2,1,0:T(8,128)(2,1)S(1)}, bf16[2,512,512]{2,1,0:T(8,128)(2,1)S(1)}, u32[]{:S(2)}, u32[]{:S(2)}) collective-permute-start(bf16[2,512,512]{2,1,0:T(8,128)(2,1)S(1)} %bitcast.66), channel_id=1, source_target_pairs={{0,256},{128,384},{256,0},{384,128},{1,257},{129,385},{257,1},{385... | collective-permute-start | bytes 3145736 | tf_op jit(solution)/shard_map/ppermute | solution.py:180
  157.1 15.1 %collective-permute-done.10 = bf16[2,512,512]{2,1,0:T(8,128)(2,1)S(1)} collective-permute-done((bf16[2,512,512]{2,1,0:T(8,128)(2,1)S(1)}, bf16[2,512,512]{2,1,0:T(8,128)(2,1)S(1)}, u32[]{:S(2)}, u32[]{:S(2)}) %collective-permute-start.10) | collective-permute-done | bytes 1048608 | tf_op jit(solution)/shard_map/ppermute | solution.py:180
  172.9 26.6 %collective-permute-done.11 = bf16[2,512,512]{2,1,0:T(8,128)(2,1)S(1)} collective-permute-done((bf16[2,512,512]{2,1,0:T(8,128)(2,1)S(1)}, bf16[2,512,512]{2,1,0:T(8,128)(2,1)S(1)}, u32[]{:S(2)}, u32[]{:S(2)}) %collective-permute-start.11) | collective-permute-done | bytes 1048608 | tf_op jit(solution)/shard_map/ppermute | solution.py:180
  (34 shorter events, 7.5 us)
Async XLA Ops:
  1.9 22.0 %all-to-all-start = ((bf16[64,8,256]{2,1,0:T(8,128)(2,1)}), bf16[64,8,256]{2,1,0:T(8,128)(2,1)S(1)}, u32[]{:S(2)}, u32[]{:S(2)}) async-start(bf16[64,8,256]{2,1,0:T(8,128)(2,1)} %bitcast.70), calls=%async_computation | async-start | bytes 524288 | tf_op jit(solution)/shard_map/all_to_all | solution.py:194
  21.7 17.6 %copy-start.2 = (bf16[512,64]{0,1:T(8,128)(2,1)S(1)}, bf16[512,64]{0,1:T(8,128)(2,1)}, u32[]{:S(2)}) copy-start(bf16[512,64]{0,1:T(8,128)(2,1)} %param.11) | copy-start | bytes 196612
  23.9 0.7 copy-start.1
  30.8 18.3 %all-to-all-start.1 = ((bf16[64,8,256]{2,1,0:T(8,128)(2,1)}), bf16[64,8,256]{2,1,0:T(8,128)(2,1)S(1)}, u32[]{:S(2)}, u32[]{:S(2)}) async-start(bf16[64,8,256]{2,1,0:T(8,128)(2,1)} %causal_conv.1), calls=%async_computation.1 | async-start | bytes 524288 | tf_op jit(solution)/shard_map/all_to_all | solution.py:206
  39.3 0.7 collective-permute-start.8
  50.2 92.2 %all-to-all-start.2 = ((bf16[16,64,512]{2,1,0:T(8,128)(2,1)}), bf16[16,64,512]{2,1,0:T(8,128)(2,1)S(1)}, u32[]{:S(2)}, u32[]{:S(2)}) async-start(bf16[16,64,512]{2,1,0:T(8,128)(2,1)} %broadcast_in_dim.2), calls=%async_computation.2 | async-start | bytes 2097152 | tf_op jit(solution)/shard_map/all_to_all | solution.py:198
  58.3 98.0 %copy-start = (bf16[256,512]{1,0:T(8,128)(2,1)S(1)}, bf16[256,512]{1,0:T(8,128)(2,1)}, u32[]{:S(2)}) copy-start(bf16[256,512]{1,0:T(8,128)(2,1)} %param.9) | copy-start | bytes 786436
  59.4 64.4 %collective-permute-start = (bf16[512,256]{1,0:T(8,128)(2,1)S(1)}, bf16[512,256]{1,0:T(8,128)(2,1)S(1)}, u32[]{:S(2)}, u32[]{:S(2)}) collective-permute-start(bf16[512,256]{1,0:T(8,128)(2,1)S(1)} %fusion.11), channel_id=1, source_target_pairs={{0,2},{2,4},{4,6},{6,0},{1,3},{3,5},{5,7},{7,1},{8,10},{10,12},{12... | collective-permute-start | bytes 786440 | tf_op jit(solution)/shard_map/ppermute | solution.py:180
  76.3 49.4 %collective-permute-start.2 = (bf16[512,256]{1,0:T(8,128)(2,1)S(1)}, bf16[512,256]{1,0:T(8,128)(2,1)S(1)}, u32[]{:S(2)}, u32[]{:S(2)}) collective-permute-start(bf16[512,256]{1,0:T(8,128)(2,1)S(1)} %fusion.11), channel_id=1, source_target_pairs={{0,6},{2,0},{4,2},{6,4},{1,7},{3,1},{5,3},{7,5},{8,14},{10,8},{12,... | collective-permute-start | bytes 786440 | tf_op jit(solution)/shard_map/ppermute | solution.py:180
  123.8 16.2 %collective-permute-start.1 = (bf16[256,256]{1,0:T(8,128)(2,1)S(1)}, bf16[256,256]{1,0:T(8,128)(2,1)S(1)}, u32[]{:S(2)}, u32[]{:S(2)}) collective-permute-start(bf16[256,256]{1,0:T(8,128)(2,1)S(1)} %slice.42), channel_id=1, source_target_pairs={{0,2},{2,4},{4,6},{6,0},{1,3},{3,5},{5,7},{7,1},{8,10},{10,12},{12... | collective-permute-start | bytes 393224 | tf_op jit(solution)/shard_map/ppermute | solution.py:180
  125.8 14.2 %collective-permute-start.3 = (bf16[256,256]{1,0:T(8,128)(2,1)S(1)}, bf16[256,256]{1,0:T(8,128)(2,1)S(1)}, u32[]{:S(2)}, u32[]{:S(2)}) collective-permute-start(bf16[256,256]{1,0:T(8,128)(2,1)S(1)} %slice.43), channel_id=1, source_target_pairs={{0,6},{2,0},{4,2},{6,4},{1,7},{3,1},{5,3},{7,5},{8,14},{10,8},{12,... | collective-permute-start | bytes 393224 | tf_op jit(solution)/shard_map/ppermute | solution.py:180
  133.7 13.0 %collective-permute-start.4 = (bf16[512,256]{1,0:T(8,128)(2,1)S(1)}, bf16[512,256]{1,0:T(8,128)(2,1)S(1)}, u32[]{:S(2)}, u32[]{:S(2)}) collective-permute-start(bf16[512,256]{1,0:T(8,128)(2,1)S(1)} %fusion.11), channel_id=1, source_target_pairs={{0,1},{1,0},{2,3},{3,2},{4,5},{5,4},{6,7},{7,6},{8,9},{9,8},{10,11... | collective-permute-start | bytes 786440 | tf_op jit(solution)/shard_map/ppermute | solution.py:184
  135.6 11.0 %collective-permute-start.5 = (bf16[512,256]{1,0:T(8,128)(2,1)S(1)}, bf16[512,256]{1,0:T(8,128)(2,1)S(1)}, u32[]{:S(2)}, u32[]{:S(2)}) collective-permute-start(bf16[512,256]{1,0:T(8,128)(2,1)S(1)} %collective-permute-done), channel_id=1, source_target_pairs={{0,1},{1,0},{2,3},{3,2},{4,5},{5,4},{6,7},{7,6},{8,9},{9,8},{10,11... | collective-permute-start | bytes 786440 | tf_op jit(solution)/shard_map/ppermute | solution.py:184
  138.0 8.6 %collective-permute-start.7 = (bf16[512,256]{1,0:T(8,128)(2,1)S(1)}, bf16[512,256]{1,0:T(8,128)(2,1)S(1)}, u32[]{:S(2)}, u32[]{:S(2)}) collective-permute-start(bf16[512,256]{1,0:T(8,128)(2,1)S(1)} %collective-permute-done.2), channel_id=1, source_target_pairs={{0,1},{1,0},{2,3},{3,2},{4,5},{5,4},{6,7},{7,6},{8,9},{9,8},{10,11... | collective-permute-start | bytes 786440 | tf_op jit(solution)/shard_map/ppermute | solution.py:184
  140.0 6.7 %collective-permute-start.6 = (bf16[512,256]{1,0:T(8,128)(2,1)S(1)}, bf16[512,256]{1,0:T(8,128)(2,1)S(1)}, u32[]{:S(2)}, u32[]{:S(2)}) collective-permute-start(bf16[512,256]{1,0:T(8,128)(2,1)S(1)} %constant_dynamic-update-slice_fusion), channel_id=1, source_target_pairs={{0,1},{1,0},{2,3},{3,2},{4,5},{5,4},{6,7},{7,6},{8,9},{9,8},{10,11... | collective-permute-start | bytes 786440 | tf_op jit(solution)/shard_map/ppermute | solution.py:184
  142.5 29.8 %collective-permute-start.10 = (bf16[2,512,512]{2,1,0:T(8,128)(2,1)S(1)}, bf16[2,512,512]{2,1,0:T(8,128)(2,1)S(1)}, u32[]{:S(2)}, u32[]{:S(2)}) collective-permute-start(bf16[2,512,512]{2,1,0:T(8,128)(2,1)S(1)} %bitcast.64), channel_id=1, source_target_pairs={{0,384},{128,0},{256,128},{384,256},{1,385},{129,1},{257,129},{385... | collective-permute-start | bytes 3145736 | tf_op jit(solution)/shard_map/ppermute | solution.py:180
  146.8 53.4 %collective-permute-start.9 = (bf16[2,512,512]{2,1,0:T(8,128)(2,1)S(1)}, bf16[2,512,512]{2,1,0:T(8,128)(2,1)S(1)}, u32[]{:S(2)}, u32[]{:S(2)}) collective-permute-start(bf16[2,512,512]{2,1,0:T(8,128)(2,1)S(1)} %bitcast.65), channel_id=1, source_target_pairs={{0,128},{128,256},{256,384},{384,0},{1,129},{129,257},{257,385},{3... | collective-permute-start | bytes 3145736 | tf_op jit(solution)/shard_map/ppermute | solution.py:180
  150.5 49.1 %collective-permute-start.11 = (bf16[2,512,512]{2,1,0:T(8,128)(2,1)S(1)}, bf16[2,512,512]{2,1,0:T(8,128)(2,1)S(1)}, u32[]{:S(2)}, u32[]{:S(2)}) collective-permute-start(bf16[2,512,512]{2,1,0:T(8,128)(2,1)S(1)} %bitcast.66), channel_id=1, source_target_pairs={{0,256},{128,384},{256,0},{384,128},{1,257},{129,385},{257,1},{385... | collective-permute-start | bytes 3145736 | tf_op jit(solution)/shard_map/ppermute | solution.py:180

commit v2 on v1

--- a/solution.py
+++ b/solution.py
@@ -194,9 +194,16 @@
     sent = lax.all_to_all(mixed, SEQ, 0, 0, tiled=True)
 
     block = lax.ppermute(w_out.T, ALL, weight_pairs())
-    block = jnp.broadcast_to(block[None], (16, 64, 512))
-    row = lax.all_to_all(block, ("x", "zl"), 0, 0, tiled=True)
-    row = row.reshape(2, 512, 512)
+
+    def gathered(part, axis):
+        pieces = [part]
+        for s in (1, 2, 3):
+            pieces.append(rotate(part, axis, s))
+        pieces, here = jnp.stack(pieces), lax.axis_index(axis)
+        return jnp.stack([take(pieces, (here - i) & 3) for i in range(4)])
+
+    row = gathered(block, "zl").reshape(256, 512)
+    row = gathered(row, "x").reshape(2, 512, 512)
     weights = [row]
     for s in (1, -1, 2):
         weights.append(rotate(row, "y", s))

time: 203 us -> 182 us (0.90)
  the two profiles are of different devices: /device:TPU:34 before, /device:TPU:99 now
where the time goes in v2:
time: 182 us; the launch traced here: 181 us
  starting transfers between devices  91.1 us (50%)
  waiting for transfers between devices  63.1 us (35%)
  Pallas kernels  16.1 us (9%)
  matrix products  5.69 us (3%)
  local copies, waits for them, and re-layouts  3.52 us (2%)
    ppermute x13, waiting for transfers between devices, rotate(): return lax.ppermute(values, axis, [(i, (i + shift) % 4) for i in range(4)])  63.1 us
    ppermute x13, starting transfers between devices, rotate(): return lax.ppermute(values, axis, [(i, (i + shift) % 4) for i in range(4)])  47.4 us
    all_to_all x1, starting transfers between devices, step(): conv = lax.all_to_all(conv, SEQ, 0, 0, tiled=True).reshape(512, B)  19 us
    all_to_all x1, starting transfers between devices, step(): sent = lax.all_to_all(mixed, SEQ, 0, 0, tiled=True)  10.2 us
    ppermute x4, starting transfers between devices, swap(): return lax.ppermute(values, 'c', [(0, 1), (1, 0)])  9.8 us
    pallas_call x1, Pallas kernels, causal_conv(): pl.pallas_call(conv_kernel, out_shape=jax.ShapeDtypeStruct((N, 8, B), jnp...  6.26 us
    pallas_call x1, Pallas kernels, prep(): pl.pallas_call(prep_kernel, out_shape=jax.ShapeDtypeStruct((8, 4, 16, 16,...  6.17 us
    dot_general x8, matrix products, step(): lax.dot_general(part, rows[core], (((0,), (1,)), ((), ())), preferred_ele...  5.69 us
  transfers between devices with their start and end apart: 20, of which 6 were waited for; matrix products, arithmetic and copies ran while one was open for 4% of the time, Pallas kernels for 8%

profile of v2, /device:TPU:99, one launch (start us, length us, event | category | flops | bytes accessed | tf_op | source)
XLA Modules:
  0.0 180.7 jit_solution(15094584328022922718)
XLA Ops:
  1.9 10.2 %all-to-all-start = ((bf16[64,8,256]{2,1,0:T(8,128)(2,1)}), bf16[64,8,256]{2,1,0:T(8,128)(2,1)S(1)}, u32[]{:S(2)}, u32[]{:S(2)}) async-start(bf16[64,8,256]{2,1,0:T(8,128)(2,1)} %bitcast.76), calls=%async_computation | async-start | bytes 524288 | tf_op jit(solution)/shard_map/all_to_all | solution.py:194
  12.0 4.8 %collective-permute-start.8 = (bf16[64,512]{1,0:T(8,128)(2,1)}, bf16[64,512]{1,0:T(8,128)(2,1)S(1)}, u32[]{:S(2)}, u32[]{:S(2)}) collective-permute-start(bf16[64,512]{1,0:T(8,128)(2,1)} %bitcast.100), channel_id=1, source_target_pairs={{0,0},{1,64},{2,128},{3,192},{4,256},{5,320},{6,384},{7,448},{8,8}... | collective-permute-start | bytes 196616 | tf_op jit(solution)/shard_map/ppermute | solution.py:196
  18.9 6.2 %prep.1.refs_1_ = bf16[8,4,16,16,256]{4,3,2,1,0:T(8,128)(2,1)} custom-call(f32[8,64,256]{2,1,0:T(8,128)} %bitcast.73), custom_call_target="tpu_custom_call" | custom-call | flops 67108864 | bytes 4194304 | tf_op jit(solution)/shard_map/prep/pallas_call | solution.py:53
  25.1 2.2 %collective-permute-start.9 = (bf16[64,512]{1,0:T(8,128)(2,1)S(1)}, bf16[64,512]{1,0:T(8,128)(2,1)S(1)}, u32[]{:S(2)}, u32[]{:S(2)}) collective-permute-start(bf16[64,512]{1,0:T(8,128)(2,1)S(1)} %collective-permute-done.8), channel_id=1, source_target_pairs={{0,8},{8,16},{16,24},{24,0},{1,9},{9,17},{17,25},{25,1},{2,10},{10... | collective-permute-start | bytes 196616 | tf_op jit(solution)/shard_map/ppermute | solution.py:180
  27.2 3.1 %collective-permute-start.10 = (bf16[64,512]{1,0:T(8,128)(2,1)S(1)}, bf16[64,512]{1,0:T(8,128)(2,1)S(1)}, u32[]{:S(2)}, u32[]{:S(2)}) collective-permute-start(bf16[64,512]{1,0:T(8,128)(2,1)S(1)} %collective-permute-done.8), channel_id=1, source_target_pairs={{0,16},{8,24},{16,0},{24,8},{1,17},{9,25},{17,1},{25,9},{2,18},{10... | collective-permute-start | bytes 196616 | tf_op jit(solution)/shard_map/ppermute | solution.py:180
  30.3 2.2 %collective-permute-start.11 = (bf16[64,512]{1,0:T(8,128)(2,1)S(1)}, bf16[64,512]{1,0:T(8,128)(2,1)S(1)}, u32[]{:S(2)}, u32[]{:S(2)}) collective-permute-start(bf16[64,512]{1,0:T(8,128)(2,1)S(1)} %collective-permute-done.8), channel_id=1, source_target_pairs={{0,24},{8,0},{16,8},{24,16},{1,25},{9,1},{17,9},{25,17},{2,26},{10... | collective-permute-start | bytes 196616 | tf_op jit(solution)/shard_map/ppermute | solution.py:180
  33.3 6.3 %causal_conv.1 = bf16[64,8,256]{2,1,0:T(8,128)(2,1)} custom-call(bf16[64,8,256]{2,1,0:T(8,128)(2,1)} %copy-done.2, bf16[8,4,16,16,256]{4,3,2,1,0:T(8,128)(2,1)} %prep.1.refs_1_), custom_call_target="tpu_custom_call" | custom-call | flops 4294967296 | bytes 4194304 | tf_op jit(solution)/shard_map/causal_conv/pallas_call | solution.py:127
  39.5 19.0 %all-to-all-start.1 = ((bf16[64,8,256]{2,1,0:T(8,128)(2,1)}), bf16[64,8,256]{2,1,0:T(8,128)(2,1)S(1)}, u32[]{:S(2)}, u32[]{:S(2)}) async-start(bf16[64,8,256]{2,1,0:T(8,128)(2,1)} %causal_conv.1), calls=%async_computation.1 | async-start | bytes 524288 | tf_op jit(solution)/shard_map/all_to_all | solution.py:213
  58.6 3.1 %collective-permute-start.12 = (bf16[256,512]{1,0:T(8,128)(2,1)S(1)}, bf16[256,512]{1,0:T(8,128)(2,1)S(1)}, u32[]{:S(2)}, u32[]{:S(2)}) collective-permute-start(bf16[256,512]{1,0:T(8,128)(2,1)S(1)} %bitcast.81), channel_id=1, source_target_pairs={{0,32},{32,64},{64,96},{96,0},{1,33},{33,65},{65,97},{97,1},{2,34}... | collective-permute-start | bytes 786440 | tf_op jit(solution)/shard_map/ppermute | solution.py:180
  61.7 2.8 %collective-permute-start.13 = (bf16[256,512]{1,0:T(8,128)(2,1)S(1)}, bf16[256,512]{1,0:T(8,128)(2,1)S(1)}, u32[]{:S(2)}, u32[]{:S(2)}) collective-permute-start(bf16[256,512]{1,0:T(8,128)(2,1)S(1)} %bitcast.82), channel_id=1, source_target_pairs={{0,64},{32,96},{64,0},{96,32},{1,65},{33,97},{65,1},{97,33},{2,66}... | collective-permute-start | bytes 786440 | tf_op jit(solution)/shard_map/ppermute | solution.py:180
  64.5 3.7 %collective-permute-start.14 = (bf16[256,512]{1,0:T(8,128)(2,1)S(1)}, bf16[256,512]{1,0:T(8,128)(2,1)S(1)}, u32[]{:S(2)}, u32[]{:S(2)}) collective-permute-start(bf16[256,512]{1,0:T(8,128)(2,1)S(1)} %bitcast.83), channel_id=1, source_target_pairs={{0,96},{32,0},{64,32},{96,64},{1,97},{33,1},{65,33},{97,65},{2,98}... | collective-permute-start | bytes 786440 | tf_op jit(solution)/shard_map/ppermute | solution.py:180
  71.3 7.6 %collective-permute-done.14 = bf16[256,512]{1,0:T(8,128)(2,1)S(1)} collective-permute-done((bf16[256,512]{1,0:T(8,128)(2,1)S(1)}, bf16[256,512]{1,0:T(8,128)(2,1)S(1)}, u32[]{:S(2)}, u32[]{:S(2)}) %collective-permute-start.14) | collective-permute-done | bytes 262176 | tf_op jit(solution)/shard_map/ppermute | solution.py:180
  79.3 4.6 %collective-permute-start.16 = (bf16[2,512,512]{2,1,0:T(8,128)(2,1)S(1)}, bf16[2,512,512]{2,1,0:T(8,128)(2,1)}, u32[]{:S(2)}, u32[]{:S(2)}) collective-permute-start(bf16[2,512,512]{2,1,0:T(8,128)(2,1)S(1)} %bitcast.77), channel_id=1, source_target_pairs={{0,384},{128,0},{256,128},{384,256},{1,385},{129,1},{257,129},{385... | collective-permute-start | bytes 3145736 | tf_op jit(solution)/shard_map/ppermute | solution.py:180
  84.0 3.1 %collective-permute-start = (bf16[512,256]{1,0:T(8,128)(2,1)S(1)}, bf16[512,256]{1,0:T(8,128)(2,1)S(1)}, u32[]{:S(2)}, u32[]{:S(2)}) collective-permute-start(bf16[512,256]{1,0:T(8,128)(2,1)S(1)} %fusion.11), channel_id=1, source_target_pairs={{0,2},{2,4},{4,6},{6,0},{1,3},{3,5},{5,7},{7,1},{8,10},{10,12},{12... | collective-permute-start | bytes 786440 | tf_op jit(solution)/shard_map/ppermute | solution.py:180
  87.1 6.1 %collective-permute-start.2 = (bf16[512,256]{1,0:T(8,128)(2,1)S(1)}, bf16[512,256]{1,0:T(8,128)(2,1)S(1)}, u32[]{:S(2)}, u32[]{:S(2)}) collective-permute-start(bf16[512,256]{1,0:T(8,128)(2,1)S(1)} %fusion.11), channel_id=1, source_target_pairs={{0,6},{2,0},{4,2},{6,4},{1,7},{3,1},{5,3},{7,5},{8,14},{10,8},{12,... | collective-permute-start | bytes 786440 | tf_op jit(solution)/shard_map/ppermute | solution.py:180
  93.2 19.0 %collective-permute-done = bf16[512,256]{1,0:T(8,128)(2,1)S(1)} collective-permute-done((bf16[512,256]{1,0:T(8,128)(2,1)S(1)}, bf16[512,256]{1,0:T(8,128)(2,1)S(1)}, u32[]{:S(2)}, u32[]{:S(2)}) %collective-permute-start) | collective-permute-done | bytes 262176 | tf_op jit(solution)/shard_map/ppermute | solution.py:180
  112.2 5.7 %collective-permute-start.1 = (bf16[256,256]{1,0:T(8,128)(2,1)S(1)}, bf16[256,256]{1,0:T(8,128)(2,1)S(1)}, u32[]{:S(2)}, u32[]{:S(2)}) collective-permute-start(bf16[256,256]{1,0:T(8,128)(2,1)S(1)} %slice.38), channel_id=1, source_target_pairs={{0,2},{2,4},{4,6},{6,0},{1,3},{3,5},{5,7},{7,1},{8,10},{10,12},{12... | collective-permute-start | bytes 393224 | tf_op jit(solution)/shard_map/ppermute | solution.py:180
  117.9 3.0 %collective-permute-start.4 = (bf16[512,256]{1,0:T(8,128)(2,1)S(1)}, bf16[512,256]{1,0:T(8,128)(2,1)S(1)}, u32[]{:S(2)}, u32[]{:S(2)}) collective-permute-start(bf16[512,256]{1,0:T(8,128)(2,1)S(1)} %fusion.11), channel_id=1, source_target_pairs={{0,1},{1,0},{2,3},{3,2},{4,5},{5,4},{6,7},{7,6},{8,9},{9,8},{10,11... | collective-permute-start | bytes 786440 | tf_op jit(solution)/shard_map/ppermute | solution.py:184
  121.6 6.6 %collective-permute-start.3 = (bf16[256,256]{1,0:T(8,128)(2,1)}, bf16[256,256]{1,0:T(8,128)(2,1)S(1)}, u32[]{:S(2)}, u32[]{:S(2)}) collective-permute-start(bf16[256,256]{1,0:T(8,128)(2,1)} %slice.39), channel_id=1, source_target_pairs={{0,6},{2,0},{4,2},{6,4},{1,7},{3,1},{5,3},{7,5},{8,14},{10,8},{12,... | collective-permute-start | bytes 393224 | tf_op jit(solution)/shard_map/ppermute | solution.py:180
  128.2 2.3 %collective-permute-start.17 = (bf16[2,512,512]{2,1,0:T(8,128)(2,1)S(1)}, bf16[2,512,512]{2,1,0:T(8,128)(2,1)S(1)}, u32[]{:S(2)}, u32[]{:S(2)}) collective-permute-start(bf16[2,512,512]{2,1,0:T(8,128)(2,1)S(1)} %bitcast.78), channel_id=1, source_target_pairs={{0,256},{128,384},{256,0},{384,128},{1,257},{129,385},{257,1},{385... | collective-permute-start | bytes 3145736 | tf_op jit(solution)/shard_map/ppermute | solution.py:180
  130.5 2.5 %collective-permute-start.5 = (bf16[512,256]{1,0:T(8,128)(2,1)S(1)}, bf16[512,256]{1,0:T(8,128)(2,1)S(1)}, u32[]{:S(2)}, u32[]{:S(2)}) collective-permute-start(bf16[512,256]{1,0:T(8,128)(2,1)S(1)} %collective-permute-done), channel_id=1, source_target_pairs={{0,1},{1,0},{2,3},{3,2},{4,5},{5,4},{6,7},{7,6},{8,9},{9,8},{10,11... | collective-permute-start | bytes 786440 | tf_op jit(solution)/shard_map/ppermute | solution.py:184
  135.2 2.3 %collective-permute-start.7 = (bf16[512,256]{1,0:T(8,128)(2,1)S(1)}, bf16[512,256]{1,0:T(8,128)(2,1)S(1)}, u32[]{:S(2)}, u32[]{:S(2)}) collective-permute-start(bf16[512,256]{1,0:T(8,128)(2,1)S(1)} %collective-permute-done.2), channel_id=1, source_target_pairs={{0,1},{1,0},{2,3},{3,2},{4,5},{5,4},{6,7},{7,6},{8,9},{9,8},{10,11... | collective-permute-start | bytes 786440 | tf_op jit(solution)/shard_map/ppermute | solution.py:184
  144.7 11.4 %collective-permute-done.17 = bf16[2,512,512]{2,1,0:T(8,128)(2,1)S(1)} collective-permute-done((bf16[2,512,512]{2,1,0:T(8,128)(2,1)S(1)}, bf16[2,512,512]{2,1,0:T(8,128)(2,1)S(1)}, u32[]{:S(2)}, u32[]{:S(2)}) %collective-permute-start.17) | collective-permute-done | bytes 1048608 | tf_op jit(solution)/shard_map/ppermute | solution.py:180
  157.6 21.6 %collective-permute-done.15 = bf16[2,512,512]{2,1,0:T(8,128)(2,1)S(1)} collective-permute-done((bf16[2,512,512]{2,1,0:T(8,128)(2,1)S(1)}, bf16[2,512,512]{2,1,0:T(8,128)(2,1)S(1)}, u32[]{:S(2)}, u32[]{:S(2)}) %collective-permute-start.15) | collective-permute-done | bytes 1048608 | tf_op jit(solution)/shard_map/ppermute | solution.py:180
  (49 shorter events, 21.0 us)
Async XLA Ops:
  1.9 30.7 %all-to-all-start = ((bf16[64,8,256]{2,1,0:T(8,128)(2,1)}), bf16[64,8,256]{2,1,0:T(8,128)(2,1)S(1)}, u32[]{:S(2)}, u32[]{:S(2)}) async-start(bf16[64,8,256]{2,1,0:T(8,128)(2,1)} %bitcast.76), calls=%async_computation | async-start | bytes 524288 | tf_op jit(solution)/shard_map/all_to_all | solution.py:194
  12.0 13.0 %collective-permute-start.8 = (bf16[64,512]{1,0:T(8,128)(2,1)}, bf16[64,512]{1,0:T(8,128)(2,1)S(1)}, u32[]{:S(2)}, u32[]{:S(2)}) collective-permute-start(bf16[64,512]{1,0:T(8,128)(2,1)} %bitcast.100), channel_id=1, source_target_pairs={{0,0},{1,64},{2,128},{3,192},{4,256},{5,320},{6,384},{7,448},{8,8}... | collective-permute-start | bytes 196616 | tf_op jit(solution)/shard_map/ppermute | solution.py:196
  25.1 33.4 %collective-permute-start.9 = (bf16[64,512]{1,0:T(8,128)(2,1)S(1)}, bf16[64,512]{1,0:T(8,128)(2,1)S(1)}, u32[]{:S(2)}, u32[]{:S(2)}) collective-permute-start(bf16[64,512]{1,0:T(8,128)(2,1)S(1)} %collective-permute-done.8), channel_id=1, source_target_pairs={{0,8},{8,16},{16,24},{24,0},{1,9},{9,17},{17,25},{25,1},{2,10},{10... | collective-permute-start | bytes 196616 | tf_op jit(solution)/shard_map/ppermute | solution.py:180
  27.2 31.3 %collective-permute-start.10 = (bf16[64,512]{1,0:T(8,128)(2,1)S(1)}, bf16[64,512]{1,0:T(8,128)(2,1)S(1)}, u32[]{:S(2)}, u32[]{:S(2)}) collective-permute-start(bf16[64,512]{1,0:T(8,128)(2,1)S(1)} %collective-permute-done.8), channel_id=1, source_target_pairs={{0,16},{8,24},{16,0},{24,8},{1,17},{9,25},{17,1},{25,9},{2,18},{10... | collective-permute-start | bytes 196616 | tf_op jit(solution)/shard_map/ppermute | solution.py:180
  30.3 28.2 %collective-permute-start.11 = (bf16[64,512]{1,0:T(8,128)(2,1)S(1)}, bf16[64,512]{1,0:T(8,128)(2,1)S(1)}, u32[]{:S(2)}, u32[]{:S(2)}) collective-permute-start(bf16[64,512]{1,0:T(8,128)(2,1)S(1)} %collective-permute-done.8), channel_id=1, source_target_pairs={{0,24},{8,0},{16,8},{24,16},{1,25},{9,1},{17,9},{25,17},{2,26},{10... | collective-permute-start | bytes 196616 | tf_op jit(solution)/shard_map/ppermute | solution.py:180
  32.5 0.7 copy-start.2
  39.5 44.4 %all-to-all-start.1 = ((bf16[64,8,256]{2,1,0:T(8,128)(2,1)}), bf16[64,8,256]{2,1,0:T(8,128)(2,1)S(1)}, u32[]{:S(2)}, u32[]{:S(2)}) async-start(bf16[64,8,256]{2,1,0:T(8,128)(2,1)} %causal_conv.1), calls=%async_computation.1 | async-start | bytes 524288 | tf_op jit(solution)/shard_map/all_to_all | solution.py:213
  58.6 11.4 %collective-permute-start.12 = (bf16[256,512]{1,0:T(8,128)(2,1)S(1)}, bf16[256,512]{1,0:T(8,128)(2,1)S(1)}, u32[]{:S(2)}, u32[]{:S(2)}) collective-permute-start(bf16[256,512]{1,0:T(8,128)(2,1)S(1)} %bitcast.81), channel_id=1, source_target_pairs={{0,32},{32,64},{64,96},{96,0},{1,33},{33,65},{65,97},{97,1},{2,34}... | collective-permute-start | bytes 786440 | tf_op jit(solution)/shard_map/ppermute | solution.py:180
  61.7 9.6 %collective-permute-start.13 = (bf16[256,512]{1,0:T(8,128)(2,1)S(1)}, bf16[256,512]{1,0:T(8,128)(2,1)S(1)}, u32[]{:S(2)}, u32[]{:S(2)}) collective-permute-start(bf16[256,512]{1,0:T(8,128)(2,1)S(1)} %bitcast.82), channel_id=1, source_target_pairs={{0,64},{32,96},{64,0},{96,32},{1,65},{33,97},{65,1},{97,33},{2,66}... | collective-permute-start | bytes 786440 | tf_op jit(solution)/shard_map/ppermute | solution.py:180
  64.5 14.4 %collective-permute-start.14 = (bf16[256,512]{1,0:T(8,128)(2,1)S(1)}, bf16[256,512]{1,0:T(8,128)(2,1)S(1)}, u32[]{:S(2)}, u32[]{:S(2)}) collective-permute-start(bf16[256,512]{1,0:T(8,128)(2,1)S(1)} %bitcast.83), channel_id=1, source_target_pairs={{0,96},{32,0},{64,32},{96,64},{1,97},{33,1},{65,33},{97,65},{2,98}... | collective-permute-start | bytes 786440 | tf_op jit(solution)/shard_map/ppermute | solution.py:180
  70.0 13.9 %copy-start = (bf16[512,256]{1,0:T(8,128)(2,1)S(1)}, bf16[512,256]{1,0:T(8,128)(2,1)}, u32[]{:S(2)}) copy-start(bf16[512,256]{1,0:T(8,128)(2,1)} %shard_map.64) | copy-start | bytes 786436
  79.3 62.6 %collective-permute-start.16 = (bf16[2,512,512]{2,1,0:T(8,128)(2,1)S(1)}, bf16[2,512,512]{2,1,0:T(8,128)(2,1)}, u32[]{:S(2)}, u32[]{:S(2)}) collective-permute-start(bf16[2,512,512]{2,1,0:T(8,128)(2,1)S(1)} %bitcast.77), channel_id=1, source_target_pairs={{0,384},{128,0},{256,128},{384,256},{1,385},{129,1},{257,129},{385... | collective-permute-start | bytes 3145736 | tf_op jit(solution)/shard_map/ppermute | solution.py:180
  84.0 28.2 %collective-permute-start = (bf16[512,256]{1,0:T(8,128)(2,1)S(1)}, bf16[512,256]{1,0:T(8,128)(2,1)S(1)}, u32[]{:S(2)}, u32[]{:S(2)}) collective-permute-start(bf16[512,256]{1,0:T(8,128)(2,1)S(1)} %fusion.11), channel_id=1, source_target_pairs={{0,2},{2,4},{4,6},{6,0},{1,3},{3,5},{5,7},{7,1},{8,10},{10,12},{12... | collective-permute-start | bytes 786440 | tf_op jit(solution)/shard_map/ppermute | solution.py:180
  87.1 33.8 %collective-permute-start.2 = (bf16[512,256]{1,0:T(8,128)(2,1)S(1)}, bf16[512,256]{1,0:T(8,128)(2,1)S(1)}, u32[]{:S(2)}, u32[]{:S(2)}) collective-permute-start(bf16[512,256]{1,0:T(8,128)(2,1)S(1)} %fusion.11), channel_id=1, source_target_pairs={{0,6},{2,0},{4,2},{6,4},{1,7},{3,1},{5,3},{7,5},{8,14},{10,8},{12,... | collective-permute-start | bytes 786440 | tf_op jit(solution)/shard_map/ppermute | solution.py:180
  112.2 18.3 %collective-permute-start.1 = (bf16[256,256]{1,0:T(8,128)(2,1)S(1)}, bf16[256,256]{1,0:T(8,128)(2,1)S(1)}, u32[]{:S(2)}, u32[]{:S(2)}) collective-permute-start(bf16[256,256]{1,0:T(8,128)(2,1)S(1)} %slice.38), channel_id=1, source_target_pairs={{0,2},{2,4},{4,6},{6,0},{1,3},{3,5},{5,7},{7,1},{8,10},{10,12},{12... | collective-permute-start | bytes 393224 | tf_op jit(solution)/shard_map/ppermute | solution.py:180
  117.9 19.7 %collective-permute-start.4 = (bf16[512,256]{1,0:T(8,128)(2,1)S(1)}, bf16[512,256]{1,0:T(8,128)(2,1)S(1)}, u32[]{:S(2)}, u32[]{:S(2)}) collective-permute-start(bf16[512,256]{1,0:T(8,128)(2,1)S(1)} %fusion.11), channel_id=1, source_target_pairs={{0,1},{1,0},{2,3},{3,2},{4,5},{5,4},{6,7},{7,6},{8,9},{9,8},{10,11... | collective-permute-start | bytes 786440 | tf_op jit(solution)/shard_map/ppermute | solution.py:184
  121.6 13.6 %collective-permute-start.3 = (bf16[256,256]{1,0:T(8,128)(2,1)}, bf16[256,256]{1,0:T(8,128)(2,1)S(1)}, u32[]{:S(2)}, u32[]{:S(2)}) collective-permute-start(bf16[256,256]{1,0:T(8,128)(2,1)} %slice.39), channel_id=1, source_target_pairs={{0,6},{2,0},{4,2},{6,4},{1,7},{3,1},{5,3},{7,5},{8,14},{10,8},{12,... | collective-permute-start | bytes 393224 | tf_op jit(solution)/shard_map/ppermute | solution.py:180
  128.2 27.9 %collective-permute-start.17 = (bf16[2,512,512]{2,1,0:T(8,128)(2,1)S(1)}, bf16[2,512,512]{2,1,0:T(8,128)(2,1)S(1)}, u32[]{:S(2)}, u32[]{:S(2)}) collective-permute-start(bf16[2,512,512]{2,1,0:T(8,128)(2,1)S(1)} %bitcast.78), channel_id=1, source_target_pairs={{0,256},{128,384},{256,0},{384,128},{1,257},{129,385},{257,1},{385... | collective-permute-start | bytes 3145736 | tf_op jit(solution)/shard_map/ppermute | solution.py:180
  130.5 9.2 %collective-permute-start.5 = (bf16[512,256]{1,0:T(8,128)(2,1)S(1)}, bf16[512,256]{1,0:T(8,128)(2,1)S(1)}, u32[]{:S(2)}, u32[]{:S(2)}) collective-permute-start(bf16[512,256]{1,0:T(8,128)(2,1)S(1)} %collective-permute-done), channel_id=1, source_target_pairs={{0,1},{1,0},{2,3},{3,2},{4,5},{5,4},{6,7},{7,6},{8,9},{9,8},{10,11... | collective-permute-start | bytes 786440 | tf_op jit(solution)/shard_map/ppermute | solution.py:184
  135.2 6.5 %collective-permute-start.7 = (bf16[512,256]{1,0:T(8,128)(2,1)S(1)}, bf16[512,256]{1,0:T(8,128)(2,1)S(1)}, u32[]{:S(2)}, u32[]{:S(2)}) collective-permute-start(bf16[512,256]{1,0:T(8,128)(2,1)S(1)} %collective-permute-done.2), channel_id=1, source_target_pairs={{0,1},{1,0},{2,3},{3,2},{4,5},{5,4},{6,7},{7,6},{8,9},{9,8},{10,11... | collective-permute-start | bytes 786440 | tf_op jit(solution)/shard_map/ppermute | solution.py:184
  137.6 4.2 %collective-permute-start.6 = (bf16[512,256]{1,0:T(8,128)(2,1)S(1)}, bf16[512,256]{1,0:T(8,128)(2,1)S(1)}, u32[]{:S(2)}, u32[]{:S(2)}) collective-permute-start(bf16[512,256]{1,0:T(8,128)(2,1)S(1)} %constant_dynamic-update-slice_fusion), channel_id=1, source_target_pairs={{0,1},{1,0},{2,3},{3,2},{4,5},{5,4},{6,7},{7,6},{8,9},{9,8},{10,11... | collective-permute-start | bytes 786440 | tf_op jit(solution)/shard_map/ppermute | solution.py:184
  139.8 39.4 %collective-permute-start.15 = (bf16[2,512,512]{2,1,0:T(8,128)(2,1)S(1)}, bf16[2,512,512]{2,1,0:T(8,128)(2,1)S(1)}, u32[]{:S(2)}, u32[]{:S(2)}) collective-permute-start(bf16[2,512,512]{2,1,0:T(8,128)(2,1)S(1)} %bitcast.79), channel_id=1, source_target_pairs={{0,128},{128,256},{256,384},{384,0},{1,129},{129,257},{257,385},{3... | collective-permute-start | bytes 3145736 | tf_op jit(solution)/shard_map/ppermute | solution.py:180
  141.8 15.1 %copy-start.1 = (bf16[256,512]{1,0:T(8,128)(2,1)S(1)}, bf16[256,512]{1,0:T(8,128)(2,1)}, u32[]{:S(2)}) copy-start(bf16[256,512]{1,0:T(8,128)(2,1)} %param.9) | copy-start | bytes 786436

commit v3 on v2

--- a/solution.py
+++ b/solution.py
@@ -25,7 +25,8 @@
 
     def channel(c, carry):
         for j in range(4):
-            x = h_ref[c, pl.ds(16 * j, 16), :]
+            halves = [h_ref[c, pl.ds(32 * j + n, 16, stride=2), :] for n in range(2)]
+            x = jnp.concatenate(halves, axis=1)
             for k in range(4):
                 n = 2**k
                 rows, chunks = (row & n) == 0, (chunk & n) == 0
@@ -58,7 +59,7 @@
         scratch_shapes=[pltpu.VMEM((16, 1024), jnp.float32)],
         cost_estimate=pl.CostEstimate(flops=2**26, bytes_accessed=2**22, transcendentals=0),
         name="prep",
-    )(h.reshape(8, N, B))
+    )(h.reshape(8, 2 * N, 128))
 
 
 def conv_body(x_ref, p_ref, o_ref, xs, gx, next_even, next_odd, *accs):
@@ -205,7 +206,7 @@
     row = gathered(block, "zl").reshape(256, 512)
     row = gathered(row, "x").reshape(2, 512, 512)
     weights = [row]
-    for s in (1, -1, 2):
+    for s in (1, 2, 3):
         weights.append(rotate(row, "y", s))
 
     taps = prep(filters)
@@ -218,19 +219,19 @@
     before = rotate(gated, "zh", -1)
     far_low = rotate(after[:256], "zh", 1)
     far_high = rotate(before[256:], "zh", -1)
-    far = jnp.concatenate([far_low, far_high], axis=0)
-    mine = jnp.stack([gated, after, far, before])
-    other = jnp.stack([swap(p) for p in (gated, after, far, before)])
+    weights = jnp.concatenate(weights, axis=0)
+
+    def product(part, r, core, low=0):
+        rows = take(weights, 2 * ((y - zh + r) & 3) + core)[:, low : low + part.shape[0]]
+        return lax.dot_general(part, rows, (((0,), (1,)), ((), ())), preferred_element_type=jnp.float32)
 
     total = stream.astype(jnp.float32)
-    for shift, rows in zip((0, 1, -1, 2), weights):
-        where = (zh - y + shift) & 3
-        pair = take(mine, where), take(other, where)
-        for core in range(2):
-            part = jnp.where(c == core, *pair)
-            total = total + lax.dot_general(
-                part, rows[core], (((0,), (1,)), ((), ())), preferred_element_type=jnp.float32
-            )
+    for r, part in ((0, gated), (1, after), (3, before)):
+        total = total + product(part, r, c)
+        total = total + product(swap(part), r, 1 - c)
+    for part, low in ((far_low, 0), (far_high, 256)):
+        total = total + product(part, 2, c, low)
+        total = total + product(swap(part), 2, 1 - c, low)
     return total.astype(jnp.bfloat16)
 
 

time: 182 us -> 174 us (0.956)
  the two profiles are of different devices: /device:TPU:99 before, /device:TPU:1 now
where the time goes in v3:
time: 174 us; the launch traced here: 173 us
  starting transfers between devices  111 us (64%)
  waiting for transfers between devices  35.2 us (20%)
  Pallas kernels  16.1 us (9%)
  matrix products  3.86 us (2%)
  other arithmetic  2.95 us (2%)
  local copies, waits for them, and re-layouts  2.85 us (2%)
    ppermute x13, starting transfers between devices, rotate(): return lax.ppermute(values, axis, [(i, (i + shift) % 4) for i in range(4)])  49.5 us
    ppermute x13, waiting for transfers between devices, rotate(): return lax.ppermute(values, axis, [(i, (i + shift) % 4) for i in range(4)])  32.4 us
    all_to_all x1, starting transfers between devices, step(): conv = lax.all_to_all(conv, SEQ, 0, 0, tiled=True).reshape(512, B)  22.7 us
    ppermute x5, starting transfers between devices, swap(): return lax.ppermute(values, 'c', [(0, 1), (1, 0)])  20.9 us
    all_to_all x1, starting transfers between devices, step(): sent = lax.all_to_all(mixed, SEQ, 0, 0, tiled=True)  12.5 us
    pallas_call x1, Pallas kernels, causal_conv(): pl.pallas_call(conv_kernel, out_shape=jax.ShapeDtypeStruct((N, 8, B), jnp...  6.26 us
    pallas_call x1, Pallas kernels, prep(): pl.pallas_call(prep_kernel, out_shape=jax.ShapeDtypeStruct((8, 4, 16, 16,...  6.17 us
    ppermute x1, starting transfers between devices, step(): block = lax.ppermute(w_out.T, ALL, weight_pairs())  5.55 us
  transfers between devices with their start and end apart: 21, of which 8 were waited for; matrix products, arithmetic and copies ran while one was open for 5% of the time, Pallas kernels for 5%

profile of v3, /device:TPU:1, one launch (start us, length us, event | category | flops | bytes accessed | tf_op | source)
XLA Modules:
  0.0 172.6 jit_solution(13862493414059600566)
XLA Ops:
  1.9 12.5 %all-to-all-start = ((bf16[64,8,256]{2,1,0:T(8,128)(2,1)}), bf16[64,8,256]{2,1,0:T(8,128)(2,1)S(1)}, u32[]{:S(2)}, u32[]{:S(2)}) async-start(bf16[64,8,256]{2,1,0:T(8,128)(2,1)} %bitcast.56), calls=%async_computation | async-start | bytes 524288 | tf_op jit(solution)/shard_map/all_to_all | solution.py:195
  14.4 5.5 %collective-permute-start = (bf16[64,512]{1,0:T(8,128)(2,1)}, bf16[64,512]{1,0:T(8,128)(2,1)S(1)}, u32[]{:S(2)}, u32[]{:S(2)}) collective-permute-start(bf16[64,512]{1,0:T(8,128)(2,1)} %bitcast.69), channel_id=1, source_target_pairs={{0,0},{1,64},{2,128},{3,192},{4,256},{5,320},{6,384},{7,448},{8,8}... | collective-permute-start | bytes 196616 | tf_op jit(solution)/shard_map/ppermute | solution.py:197
  20.0 2.8 %collective-permute-done = bf16[64,512]{1,0:T(8,128)(2,1)S(1)} collective-permute-done((bf16[64,512]{1,0:T(8,128)(2,1)}, bf16[64,512]{1,0:T(8,128)(2,1)S(1)}, u32[]{:S(2)}, u32[]{:S(2)}) %collective-permute-start) | collective-permute-done | bytes 65568 | tf_op jit(solution)/shard_map/ppermute | solution.py:197
  22.7 3.2 %collective-permute-start.1 = (bf16[64,512]{1,0:T(8,128)(2,1)S(1)}, bf16[64,512]{1,0:T(8,128)(2,1)S(1)}, u32[]{:S(2)}, u32[]{:S(2)}) collective-permute-start(bf16[64,512]{1,0:T(8,128)(2,1)S(1)} %collective-permute-done), channel_id=1, source_target_pairs={{0,8},{8,16},{16,24},{24,0},{1,9},{9,17},{17,25},{25,1},{2,10},{10... | collective-permute-start | bytes 196616 | tf_op jit(solution)/shard_map/ppermute | solution.py:181
  25.9 3.7 %collective-permute-start.2 = (bf16[64,512]{1,0:T(8,128)(2,1)S(1)}, bf16[64,512]{1,0:T(8,128)(2,1)S(1)}, u32[]{:S(2)}, u32[]{:S(2)}) collective-permute-start(bf16[64,512]{1,0:T(8,128)(2,1)S(1)} %collective-permute-done), channel_id=1, source_target_pairs={{0,16},{8,24},{16,0},{24,8},{1,17},{9,25},{17,1},{25,9},{2,18},{10... | collective-permute-start | bytes 196616 | tf_op jit(solution)/shard_map/ppermute | solution.py:181
  29.6 3.4 %collective-permute-start.3 = (bf16[64,512]{1,0:T(8,128)(2,1)S(1)}, bf16[64,512]{1,0:T(8,128)(2,1)S(1)}, u32[]{:S(2)}, u32[]{:S(2)}) collective-permute-start(bf16[64,512]{1,0:T(8,128)(2,1)S(1)} %collective-permute-done), channel_id=1, source_target_pairs={{0,24},{8,0},{16,8},{24,16},{1,25},{9,1},{17,9},{25,17},{2,26},{10... | collective-permute-start | bytes 196616 | tf_op jit(solution)/shard_map/ppermute | solution.py:181
  35.2 1.9 %collective-permute-start.5 = (bf16[256,512]{1,0:T(8,128)(2,1)S(1)}, bf16[256,512]{1,0:T(8,128)(2,1)S(1)}, u32[]{:S(2)}, u32[]{:S(2)}) collective-permute-start(bf16[256,512]{1,0:T(8,128)(2,1)S(1)} %bitcast.57), channel_id=1, source_target_pairs={{0,64},{32,96},{64,0},{96,32},{1,65},{33,97},{65,1},{97,33},{2,66}... | collective-permute-start | bytes 786440 | tf_op jit(solution)/shard_map/ppermute | solution.py:181
  37.1 5.5 %collective-permute-start.6 = (bf16[256,512]{1,0:T(8,128)(2,1)S(1)}, bf16[256,512]{1,0:T(8,128)(2,1)S(1)}, u32[]{:S(2)}, u32[]{:S(2)}) collective-permute-start(bf16[256,512]{1,0:T(8,128)(2,1)S(1)} %bitcast.58), channel_id=1, source_target_pairs={{0,96},{32,0},{64,32},{96,64},{1,97},{33,1},{65,33},{97,65},{2,98}... | collective-permute-start | bytes 786440 | tf_op jit(solution)/shard_map/ppermute | solution.py:181
  44.6 1.9 %copy.9 = f32[1,8,128,128]{3,2,1,0:T(8,128)} copy(f32[1,8,128,128]{3,1,2,0:T(8,128)} %bitcast.61) | data formatting | bytes 1048576
  46.5 6.2 %prep.1.refs_1_ = bf16[8,4,16,16,256]{4,3,2,1,0:T(8,128)(2,1)} custom-call(f32[8,128,128]{2,1,0:T(8,128)} %bitcast.55), custom_call_target="tpu_custom_call" | custom-call | flops 67108864 | bytes 4194304 | tf_op jit(solution)/shard_map/prep/pallas_call | solution.py:54
  53.6 6.3 %causal_conv.1 = bf16[64,8,256]{2,1,0:T(8,128)(2,1)} custom-call(bf16[64,8,256]{2,1,0:T(8,128)(2,1)} %copy-done, bf16[8,4,16,16,256]{4,3,2,1,0:T(8,128)(2,1)} %prep.1.refs_1_), custom_call_target="tpu_custom_call" | custom-call | flops 4294967296 | bytes 4194304 | tf_op jit(solution)/shard_map/causal_conv/pallas_call | solution.py:128
  59.9 22.7 %all-to-all-start.1 = ((bf16[64,8,256]{2,1,0:T(8,128)(2,1)}), bf16[64,8,256]{2,1,0:T(8,128)(2,1)S(1)}, u32[]{:S(2)}, u32[]{:S(2)}) async-start(bf16[64,8,256]{2,1,0:T(8,128)(2,1)} %causal_conv.1), calls=%async_computation.1 | async-start | bytes 524288 | tf_op jit(solution)/shard_map/all_to_all | solution.py:214
  82.8 2.9 %collective-permute-start.7 = (bf16[2,512,512]{2,1,0:T(8,128)(2,1)S(1)}, bf16[2,512,512]{2,1,0:T(8,128)(2,1)S(1)}, u32[]{:S(2)}, u32[]{:S(2)}) collective-permute-start(bf16[2,512,512]{2,1,0:T(8,128)(2,1)S(1)} %bitcast.51), channel_id=1, source_target_pairs={{0,128},{128,256},{256,384},{384,0},{1,129},{129,257},{257,385},{3... | collective-permute-start | bytes 3145736 | tf_op jit(solution)/shard_map/ppermute | solution.py:181
  85.8 4.5 %collective-permute-start.8 = (bf16[2,512,512]{2,1,0:T(8,128)(2,1)S(1)}, bf16[2,512,512]{2,1,0:T(8,128)(2,1)S(1)}, u32[]{:S(2)}, u32[]{:S(2)}) collective-permute-start(bf16[2,512,512]{2,1,0:T(8,128)(2,1)S(1)} %bitcast.52), channel_id=1, source_target_pairs={{0,256},{128,384},{256,0},{384,128},{1,257},{129,385},{257,1},{385... | collective-permute-start | bytes 3145736 | tf_op jit(solution)/shard_map/ppermute | solution.py:181
  90.3 3.0 %collective-permute-start.9 = (bf16[2,512,512]{2,1,0:T(8,128)(2,1)S(1)}, bf16[2,512,512]{2,1,0:T(8,128)(2,1)}, u32[]{:S(2)}, u32[]{:S(2)}) collective-permute-start(bf16[2,512,512]{2,1,0:T(8,128)(2,1)S(1)} %bitcast.53), channel_id=1, source_target_pairs={{0,384},{128,0},{256,128},{384,256},{1,385},{129,1},{257,129},{385... | collective-permute-start | bytes 3145736 | tf_op jit(solution)/shard_map/ppermute | solution.py:181
  96.0 7.7 %collective-permute-start.11 = (bf16[512,256]{1,0:T(8,128)(2,1)S(1)}, bf16[512,256]{1,0:T(8,128)(2,1)S(1)}, u32[]{:S(2)}, u32[]{:S(2)}) collective-permute-start(bf16[512,256]{1,0:T(8,128)(2,1)S(1)} %fusion.6), channel_id=1, source_target_pairs={{0,2},{2,4},{4,6},{6,0},{1,3},{3,5},{5,7},{7,1},{8,10},{10,12},{12... | collective-permute-start | bytes 786440 | tf_op jit(solution)/shard_map/ppermute | solution.py:181
  105.6 6.4 %collective-permute-done.7 = bf16[2,512,512]{2,1,0:T(8,128)(2,1)S(1)} collective-permute-done((bf16[2,512,512]{2,1,0:T(8,128)(2,1)S(1)}, bf16[2,512,512]{2,1,0:T(8,128)(2,1)S(1)}, u32[]{:S(2)}, u32[]{:S(2)}) %collective-permute-start.7) | collective-permute-done | bytes 1048608 | tf_op jit(solution)/shard_map/ppermute | solution.py:181
  112.0 23.0 %collective-permute-done.8 = bf16[2,512,512]{2,1,0:T(8,128)(2,1)S(1)} collective-permute-done((bf16[2,512,512]{2,1,0:T(8,128)(2,1)S(1)}, bf16[2,512,512]{2,1,0:T(8,128)(2,1)S(1)}, u32[]{:S(2)}, u32[]{:S(2)}) %collective-permute-start.8) | collective-permute-done | bytes 1048608 | tf_op jit(solution)/shard_map/ppermute | solution.py:181
  137.3 3.6 %collective-permute-start.10 = (bf16[512,256]{1,0:T(8,128)(2,1)S(1)}, bf16[512,256]{1,0:T(8,128)(2,1)S(1)}, u32[]{:S(2)}, u32[]{:S(2)}) collective-permute-start(bf16[512,256]{1,0:T(8,128)(2,1)S(1)} %fusion.6), channel_id=1, source_target_pairs={{0,1},{1,0},{2,3},{3,2},{4,5},{5,4},{6,7},{7,6},{8,9},{9,8},{10,11... | collective-permute-start | bytes 786440 | tf_op jit(solution)/shard_map/ppermute | solution.py:185
  141.1 8.0 %collective-permute-start.15 = (bf16[256,256]{1,0:T(8,128)(2,1)S(1)}, bf16[256,256]{1,0:T(8,128)(2,1)S(1)}, u32[]{:S(2)}, u32[]{:S(2)}) collective-permute-start(bf16[256,256]{1,0:T(8,128)(2,1)S(1)} %slice.24), channel_id=1, source_target_pairs={{0,2},{2,4},{4,6},{6,0},{1,3},{3,5},{5,7},{7,1},{8,10},{10,12},{12... | collective-permute-start | bytes 393224 | tf_op jit(solution)/shard_map/ppermute | solution.py:181
  152.1 2.2 %collective-permute-start.12 = (bf16[512,256]{1,0:T(8,128)(2,1)S(1)}, bf16[512,256]{1,0:T(8,128)(2,1)S(1)}, u32[]{:S(2)}, u32[]{:S(2)}) collective-permute-start(bf16[512,256]{1,0:T(8,128)(2,1)S(1)} %collective-permute-done.11), channel_id=1, source_target_pairs={{0,1},{1,0},{2,3},{3,2},{4,5},{5,4},{6,7},{7,6},{8,9},{9,8},{10,11... | collective-permute-start | bytes 786440 | tf_op jit(solution)/shard_map/ppermute | solution.py:185
  154.3 2.1 %collective-permute-start.14 = (bf16[512,256]{1,0:T(8,128)(2,1)S(1)}, bf16[512,256]{1,0:T(8,128)(2,1)S(1)}, u32[]{:S(2)}, u32[]{:S(2)}) collective-permute-start(bf16[512,256]{1,0:T(8,128)(2,1)S(1)} %collective-permute-done.13), channel_id=1, source_target_pairs={{0,1},{1,0},{2,3},{3,2},{4,5},{5,4},{6,7},{7,6},{8,9},{9,8},{10,11... | collective-permute-start | bytes 786440 | tf_op jit(solution)/shard_map/ppermute | solution.py:185
  156.8 5.7 %collective-permute-start.16 = (bf16[256,256]{1,0:T(8,128)(2,1)S(1)}, bf16[256,256]{1,0:T(8,128)(2,1)S(1)}, u32[]{:S(2)}, u32[]{:S(2)}) collective-permute-start(bf16[256,256]{1,0:T(8,128)(2,1)S(1)} %collective-permute-done.15), channel_id=1, source_target_pairs={{0,1},{1,0},{2,3},{3,2},{4,5},{5,4},{6,7},{7,6},{8,9},{9,8},{10,11... | collective-permute-start | bytes 393224 | tf_op jit(solution)/shard_map/ppermute | solution.py:185
  163.0 7.3 %collective-permute-start.18 = (bf16[256,256]{1,0:T(8,128)(2,1)S(1)}, bf16[256,256]{1,0:T(8,128)(2,1)S(1)}, u32[]{:S(2)}, u32[]{:S(2)}) collective-permute-start(bf16[256,256]{1,0:T(8,128)(2,1)S(1)} %collective-permute-done.17), channel_id=1, source_target_pairs={{0,1},{1,0},{2,3},{3,2},{4,5},{5,4},{6,7},{7,6},{8,9},{9,8},{10,11... | collective-permute-start | bytes 393224 | tf_op jit(solution)/shard_map/ppermute | solution.py:185
  (48 shorter events, 20.2 us)
Async XLA Ops:
  1.9 51.0 %all-to-all-start = ((bf16[64,8,256]{2,1,0:T(8,128)(2,1)}), bf16[64,8,256]{2,1,0:T(8,128)(2,1)S(1)}, u32[]{:S(2)}, u32[]{:S(2)}) async-start(bf16[64,8,256]{2,1,0:T(8,128)(2,1)} %bitcast.56), calls=%async_computation | async-start | bytes 524288 | tf_op jit(solution)/shard_map/all_to_all | solution.py:195
  14.4 8.3 %collective-permute-start = (bf16[64,512]{1,0:T(8,128)(2,1)}, bf16[64,512]{1,0:T(8,128)(2,1)S(1)}, u32[]{:S(2)}, u32[]{:S(2)}) collective-permute-start(bf16[64,512]{1,0:T(8,128)(2,1)} %bitcast.69), channel_id=1, source_target_pairs={{0,0},{1,64},{2,128},{3,192},{4,256},{5,320},{6,384},{7,448},{8,8}... | collective-permute-start | bytes 196616 | tf_op jit(solution)/shard_map/ppermute | solution.py:197
  22.7 10.3 %collective-permute-start.1 = (bf16[64,512]{1,0:T(8,128)(2,1)S(1)}, bf16[64,512]{1,0:T(8,128)(2,1)S(1)}, u32[]{:S(2)}, u32[]{:S(2)}) collective-permute-start(bf16[64,512]{1,0:T(8,128)(2,1)S(1)} %collective-permute-done), channel_id=1, source_target_pairs={{0,8},{8,16},{16,24},{24,0},{1,9},{9,17},{17,25},{25,1},{2,10},{10... | collective-permute-start | bytes 196616 | tf_op jit(solution)/shard_map/ppermute | solution.py:181
  25.9 7.7 %collective-permute-start.2 = (bf16[64,512]{1,0:T(8,128)(2,1)S(1)}, bf16[64,512]{1,0:T(8,128)(2,1)S(1)}, u32[]{:S(2)}, u32[]{:S(2)}) collective-permute-start(bf16[64,512]{1,0:T(8,128)(2,1)S(1)} %collective-permute-done), channel_id=1, source_target_pairs={{0,16},{8,24},{16,0},{24,8},{1,17},{9,25},{17,1},{25,9},{2,18},{10... | collective-permute-start | bytes 196616 | tf_op jit(solution)/shard_map/ppermute | solution.py:181
  29.6 5.5 %collective-permute-start.3 = (bf16[64,512]{1,0:T(8,128)(2,1)S(1)}, bf16[64,512]{1,0:T(8,128)(2,1)S(1)}, u32[]{:S(2)}, u32[]{:S(2)}) collective-permute-start(bf16[64,512]{1,0:T(8,128)(2,1)S(1)} %collective-permute-done), channel_id=1, source_target_pairs={{0,24},{8,0},{16,8},{24,16},{1,25},{9,1},{17,9},{25,17},{2,26},{10... | collective-permute-start | bytes 196616 | tf_op jit(solution)/shard_map/ppermute | solution.py:181
  35.2 17.5 %collective-permute-start.5 = (bf16[256,512]{1,0:T(8,128)(2,1)S(1)}, bf16[256,512]{1,0:T(8,128)(2,1)S(1)}, u32[]{:S(2)}, u32[]{:S(2)}) collective-permute-start(bf16[256,512]{1,0:T(8,128)(2,1)S(1)} %bitcast.57), channel_id=1, source_target_pairs={{0,64},{32,96},{64,0},{96,32},{1,65},{33,97},{65,1},{97,33},{2,66}... | collective-permute-start | bytes 786440 | tf_op jit(solution)/shard_map/ppermute | solution.py:181
  37.1 15.6 %collective-permute-start.6 = (bf16[256,512]{1,0:T(8,128)(2,1)S(1)}, bf16[256,512]{1,0:T(8,128)(2,1)S(1)}, u32[]{:S(2)}, u32[]{:S(2)}) collective-permute-start(bf16[256,512]{1,0:T(8,128)(2,1)S(1)} %bitcast.58), channel_id=1, source_target_pairs={{0,96},{32,0},{64,32},{96,64},{1,97},{33,1},{65,33},{97,65},{2,98}... | collective-permute-start | bytes 786440 | tf_op jit(solution)/shard_map/ppermute | solution.py:181
  42.7 10.1 %collective-permute-start.4 = (bf16[256,512]{1,0:T(8,128)(2,1)S(1)}, bf16[256,512]{1,0:T(8,128)(2,1)S(1)}, u32[]{:S(2)}, u32[]{:S(2)}) collective-permute-start(bf16[256,512]{1,0:T(8,128)(2,1)S(1)} %bitcast.59), channel_id=1, source_target_pairs={{0,32},{32,64},{64,96},{96,0},{1,33},{33,65},{65,97},{97,1},{2,34}... | collective-permute-start | bytes 786440 | tf_op jit(solution)/shard_map/ppermute | solution.py:181
  52.9 0.7 copy-start
  59.9 35.2 %all-to-all-start.1 = ((bf16[64,8,256]{2,1,0:T(8,128)(2,1)}), bf16[64,8,256]{2,1,0:T(8,128)(2,1)S(1)}, u32[]{:S(2)}, u32[]{:S(2)}) async-start(bf16[64,8,256]{2,1,0:T(8,128)(2,1)} %causal_conv.1), calls=%async_computation.1 | async-start | bytes 524288 | tf_op jit(solution)/shard_map/all_to_all | solution.py:214
  82.8 29.2 %collective-permute-start.7 = (bf16[2,512,512]{2,1,0:T(8,128)(2,1)S(1)}, bf16[2,512,512]{2,1,0:T(8,128)(2,1)S(1)}, u32[]{:S(2)}, u32[]{:S(2)}) collective-permute-start(bf16[2,512,512]{2,1,0:T(8,128)(2,1)S(1)} %bitcast.51), channel_id=1, source_target_pairs={{0,128},{128,256},{256,384},{384,0},{1,129},{129,257},{257,385},{3... | collective-permute-start | bytes 3145736 | tf_op jit(solution)/shard_map/ppermute | solution.py:181
  85.8 49.3 %collective-permute-start.8 = (bf16[2,512,512]{2,1,0:T(8,128)(2,1)S(1)}, bf16[2,512,512]{2,1,0:T(8,128)(2,1)S(1)}, u32[]{:S(2)}, u32[]{:S(2)}) collective-permute-start(bf16[2,512,512]{2,1,0:T(8,128)(2,1)S(1)} %bitcast.52), channel_id=1, source_target_pairs={{0,256},{128,384},{256,0},{384,128},{1,257},{129,385},{257,1},{385... | collective-permute-start | bytes 3145736 | tf_op jit(solution)/shard_map/ppermute | solution.py:181
  90.3 45.4 %collective-permute-start.9 = (bf16[2,512,512]{2,1,0:T(8,128)(2,1)S(1)}, bf16[2,512,512]{2,1,0:T(8,128)(2,1)}, u32[]{:S(2)}, u32[]{:S(2)}) collective-permute-start(bf16[2,512,512]{2,1,0:T(8,128)(2,1)S(1)} %bitcast.53), channel_id=1, source_target_pairs={{0,384},{128,0},{256,128},{384,256},{1,385},{129,1},{257,129},{385... | collective-permute-start | bytes 3145736 | tf_op jit(solution)/shard_map/ppermute | solution.py:181
  96.0 45.0 %collective-permute-start.11 = (bf16[512,256]{1,0:T(8,128)(2,1)S(1)}, bf16[512,256]{1,0:T(8,128)(2,1)S(1)}, u32[]{:S(2)}, u32[]{:S(2)}) collective-permute-start(bf16[512,256]{1,0:T(8,128)(2,1)S(1)} %fusion.6), channel_id=1, source_target_pairs={{0,2},{2,4},{4,6},{6,0},{1,3},{3,5},{5,7},{7,1},{8,10},{10,12},{12... | collective-permute-start | bytes 786440 | tf_op jit(solution)/shard_map/ppermute | solution.py:181
  103.7 45.3 %collective-permute-start.13 = (bf16[512,256]{1,0:T(8,128)(2,1)S(1)}, bf16[512,256]{1,0:T(8,128)(2,1)S(1)}, u32[]{:S(2)}, u32[]{:S(2)}) collective-permute-start(bf16[512,256]{1,0:T(8,128)(2,1)S(1)} %fusion.6), channel_id=1, source_target_pairs={{0,6},{2,0},{4,2},{6,4},{1,7},{3,1},{5,3},{7,5},{8,14},{10,8},{12,... | collective-permute-start | bytes 786440 | tf_op jit(solution)/shard_map/ppermute | solution.py:181
  137.3 14.4 %copy-start.1 = (bf16[256,512]{1,0:T(8,128)(2,1)S(1)}, bf16[256,512]{1,0:T(8,128)(2,1)}, u32[]{:S(2)}) copy-start(bf16[256,512]{1,0:T(8,128)(2,1)} %param.9) | copy-start | bytes 786436
  137.3 14.0 %collective-permute-start.10 = (bf16[512,256]{1,0:T(8,128)(2,1)S(1)}, bf16[512,256]{1,0:T(8,128)(2,1)S(1)}, u32[]{:S(2)}, u32[]{:S(2)}) collective-permute-start(bf16[512,256]{1,0:T(8,128)(2,1)S(1)} %fusion.6), channel_id=1, source_target_pairs={{0,1},{1,0},{2,3},{3,2},{4,5},{5,4},{6,7},{7,6},{8,9},{9,8},{10,11... | collective-permute-start | bytes 786440 | tf_op jit(solution)/shard_map/ppermute | solution.py:185
  141.1 15.7 %collective-permute-start.15 = (bf16[256,256]{1,0:T(8,128)(2,1)S(1)}, bf16[256,256]{1,0:T(8,128)(2,1)S(1)}, u32[]{:S(2)}, u32[]{:S(2)}) collective-permute-start(bf16[256,256]{1,0:T(8,128)(2,1)S(1)} %slice.24), channel_id=1, source_target_pairs={{0,2},{2,4},{4,6},{6,0},{1,3},{3,5},{5,7},{7,1},{8,10},{10,12},{12... | collective-permute-start | bytes 393224 | tf_op jit(solution)/shard_map/ppermute | solution.py:181
  149.1 13.9 %collective-permute-start.17 = (bf16[256,256]{1,0:T(8,128)(2,1)S(1)}, bf16[256,256]{1,0:T(8,128)(2,1)S(1)}, u32[]{:S(2)}, u32[]{:S(2)}) collective-permute-start(bf16[256,256]{1,0:T(8,128)(2,1)S(1)} %slice.27), channel_id=1, source_target_pairs={{0,6},{2,0},{4,2},{6,4},{1,7},{3,1},{5,3},{7,5},{8,14},{10,8},{12,... | collective-permute-start | bytes 393224 | tf_op jit(solution)/shard_map/ppermute | solution.py:181
  152.1 18.5 %collective-permute-start.12 = (bf16[512,256]{1,0:T(8,128)(2,1)S(1)}, bf16[512,256]{1,0:T(8,128)(2,1)S(1)}, u32[]{:S(2)}, u32[]{:S(2)}) collective-permute-start(bf16[512,256]{1,0:T(8,128)(2,1)S(1)} %collective-permute-done.11), channel_id=1, source_target_pairs={{0,1},{1,0},{2,3},{3,2},{4,5},{5,4},{6,7},{7,6},{8,9},{9,8},{10,11... | collective-permute-start | bytes 786440 | tf_op jit(solution)/shard_map/ppermute | solution.py:185
  154.3 16.7 %collective-permute-start.14 = (bf16[512,256]{1,0:T(8,128)(2,1)S(1)}, bf16[512,256]{1,0:T(8,128)(2,1)S(1)}, u32[]{:S(2)}, u32[]{:S(2)}) collective-permute-start(bf16[512,256]{1,0:T(8,128)(2,1)S(1)} %collective-permute-done.13), channel_id=1, source_target_pairs={{0,1},{1,0},{2,3},{3,2},{4,5},{5,4},{6,7},{7,6},{8,9},{9,8},{10,11... | collective-permute-start | bytes 786440 | tf_op jit(solution)/shard_map/ppermute | solution.py:185
  156.8 14.6 %collective-permute-start.16 = (bf16[256,256]{1,0:T(8,128)(2,1)S(1)}, bf16[256,256]{1,0:T(8,128)(2,1)S(1)}, u32[]{:S(2)}, u32[]{:S(2)}) collective-permute-start(bf16[256,256]{1,0:T(8,128)(2,1)S(1)} %collective-permute-done.15), channel_id=1, source_target_pairs={{0,1},{1,0},{2,3},{3,2},{4,5},{5,4},{6,7},{7,6},{8,9},{9,8},{10,11... | collective-permute-start | bytes 393224 | tf_op jit(solution)/shard_map/ppermute | solution.py:185
  163.0 8.7 %collective-permute-start.18 = (bf16[256,256]{1,0:T(8,128)(2,1)S(1)}, bf16[256,256]{1,0:T(8,128)(2,1)S(1)}, u32[]{:S(2)}, u32[]{:S(2)}) collective-permute-start(bf16[256,256]{1,0:T(8,128)(2,1)S(1)} %collective-permute-done.17), channel_id=1, source_target_pairs={{0,1},{1,0},{2,3},{3,2},{4,5},{5,4},{6,7},{7,6},{8,9},{9,8},{10,11... | collective-permute-start | bytes 393224 | tf_op jit(solution)/shard_map/ppermute | solution.py:185
